TPU v7x, 256 devices: a whole 4x4x8 slice. The times are simulated.
256 devices in a mesh: space: 32 (over z, x), sample: 8 (over y, core).
Axes of the slice: x: 4, y: 4, z: 8, core: 2. Of those that a mesh axis runs over, the one named last changes fastest.
Arguments:
- crops: bfloat16 [256, 16, 64, 1024], P('sample', None, 'space'), may hold values from -6 to 6
- first_kernel: bfloat16 [32, 16, 3, 3, 3], replicated, may hold values from -0.3125 to 0.3125
- second_kernel: bfloat16 [64, 32, 3, 3, 3], replicated, may hold values from -0.21875 to 0.21875
- out_grad: bfloat16 [256, 64, 16, 64], P(('sample', 'space')), may hold values from -0.03125 to 0.03125
Outputs:
- features_out: bfloat16 [256, 64, 16, 64], P(('sample', 'space'))
- first_grad: float32 [32, 16, 3, 3, 3], replicated
- second_grad: float32 [64, 32, 3, 3, 3], replicated
All inputs are finite; a program needn't handle non-finite values.
Results may differ from a plain program's by a relative error of at most 0.012.
Values may be sent and summed in bfloat16 or wider, within the bound.
A program may use at most 128 MiB of HBM per device.

v0:
```python
import jax
import jax.numpy as jnp
from jax import lax
from jax.sharding import PartitionSpec as P

HEIGHT = 8
WIDTH = 128


def forward_conv(field, kernel, depth_pad):
    return lax.conv_general_dilated(
        field,
        kernel,
        (2, 2, 2),
        (depth_pad, (1, 0), (1, 0)),
        dimension_numbers=("NCDHW", "OIDHW", "NCDHW"),
        preferred_element_type=jnp.float32,
    )


def kernel_grad(field, cotangent, depth_pad):
    return lax.conv_general_dilated(
        field,
        cotangent,
        (1, 1, 1),
        (depth_pad, (1, 0), (1, 0)),
        rhs_dilation=(2, 2, 2),
        dimension_numbers=("CNDHW", "IODHW", "CNDHW"),
        preferred_element_type=jnp.float32,
    )


def input_grad(cotangent, kernel):
    flipped = kernel[:, :, ::-1, ::-1, ::-1]
    return lax.conv_general_dilated(
        cotangent,
        flipped,
        (1, 1, 1),
        ((1, 2), (1, 2), (1, 2)),
        lhs_dilation=(2, 2, 2),
        dimension_numbers=("NCDHW", "IODHW", "NCDHW"),
        preferred_element_type=jnp.float32,
    )


def silu_slope(value):
    sigma = jax.nn.sigmoid(value)
    return sigma * (1.0 + value * (1.0 - sigma))


def body(crops, first_kernel, second_kernel, out_grad):
    local_samples, channels_in, planes, flat_cells = crops.shape
    whole_input = lax.all_to_all(crops, "space", split_axis=0, concat_axis=2, tiled=True)
    whole_input = whole_input.reshape(
        whole_input.shape[0], channels_in, whole_input.shape[2], HEIGHT, WIDTH
    )
    first_pre = forward_conv(whole_input, first_kernel, (1, 0))
    act_whole = jax.nn.silu(first_pre).astype(jnp.bfloat16)
    sample_count = act_whole.shape[0]
    second_pre = forward_conv(act_whole, second_kernel, (1, 0))
    features_out = second_pre.astype(jnp.bfloat16).reshape(out_grad.shape)
    cotangent = out_grad.reshape(
        sample_count, out_grad.shape[1], out_grad.shape[2], HEIGHT // 4, WIDTH // 4
    )
    second_grad = kernel_grad(act_whole, cotangent, (1, 0))
    act_grad = input_grad(cotangent, second_kernel).astype(jnp.bfloat16)
    pre_grad = (act_grad.astype(jnp.float32) * silu_slope(first_pre)).astype(jnp.bfloat16)
    first_grad = kernel_grad(whole_input, pre_grad, (1, 0))
    first_grad, second_grad = lax.psum((first_grad, second_grad), ("space", "sample"))
    return (features_out, first_grad, second_grad)


def solution(mesh):
    placed = (P("sample", None, "space", None), P(), P(), P(("sample", "space"), None, None, None))
    return jax.shard_map(
        body,
        mesh=mesh,
        in_specs=placed,
        out_specs=(P(("sample", "space"), None, None, None), P(), P()),
        check_vma=False,
    )
```

profile of v0, /device:TPU:1, one launch (start us, length us, event | category | flops | bytes accessed | tf_op | source)
XLA Modules:
  0.0 415.9 jit_solution(15933746394667295038)
XLA Ops:
  7.2 12.0 %all-to-all-start = ((bf16[32,16,2,1024]{3,2,1,0:T(2,128)(2,1)}), bf16[32,16,2,1024]{3,2,1,0:T(2,128)(2,1)S(1)}, u32[]{:S(2)}, u32[]{:S(2)}) async-start(bf16[32,16,2,1024]{3,2,1,0:T(2,128)(2,1)} %param.4), calls=%async_computation | async-start | bytes 4194304 | tf_op jit(solution)/shard_map/all_to_all | solution.py:53
  19.3 1.2 copy.72
  20.5 0.2 copy.91
  20.9 2.4 fusion.19
  23.3 5.4 %copy.76 = f32[32,4,8,10,32]{4,0,3,2,1:T(8,128)} copy(f32[32,4,8,10,32]{4,2,3,1,0:T(8,128)S(1)} %fusion.19) | data formatting | bytes 2621440 | tf_op jit(solution)/shard_map/convert_element_type | solution.py:67
  28.7 39.0 %all-to-all-done = bf16[32,16,2,1024]{3,2,1,0:T(2,128)(2,1)S(1)} async-done(((bf16[32,16,2,1024]{3,2,1,0:T(2,128)(2,1)}), bf16[32,16,2,1024]{3,2,1,0:T(2,128)(2,1)S(1)}, u32[]{:S(2)}, u32[]{:S(2)}) %all-to-all-start) | async-done | bytes 2097184 | tf_op jit(solution)/shard_map/all_to_all | solution.py:53
  67.7 0.7 copy.60
  68.4 0.6 copy.92
  69.0 5.3 %copy.90 = bf16[16,64,8,1,128]{1,2,4,0,3:T(8,128)(2,1)} copy(bf16[16,64,8,1,128]{4,2,0,1,3:T(8,128)(2,1)S(1)} %bitcast.48) | data formatting | bytes 4194304
  74.3 5.6 %pad.clone = bf16[16,64,8,1,144]{1,2,4,0,3:T(8,128)(2,1)} pad(bf16[16,64,8,1,128]{1,2,4,0,3:T(8,128)(2,1)} %copy.90, bf16[]{:T(256)} %constant.6), padding=0_0x0_0x0_0x0_0x1_15 | pad | bytes 4456450 | tf_op jit(solution)/shard_map/reshape | solution.py:54
  79.9 32.5 %copy.63 = bf16[16,64,8,1,8,18]{0,4,5,2,1,3:T(8,128)(2,1)} copy(bf16[16,64,8,1,8,18]{1,2,5,4,0,3:T(8,128)(2,1)} %bitcast.50) | data formatting | bytes 4718592 | tf_op jit(solution)/shard_map/conv_general_dilated | solution.py:11
  112.4 3.9 slice.9
  116.3 20.1 %broadcast_select_fusion = (bf16[32,4,8,9,32]{4,2,3,1,0:T(8,128)(2,1)}, bf16[32,4,8,9,32]{4,2,3,1,0:T(8,128)(2,1)}, f32[32,4,8,9,32]{4,2,3,1,0:T(8,128)}) fusion(pred[8,9]{0,1:T(8,128)(4,1)S(1)} %copy-done.7, bf16[32,16,3,3,3]{0,1,4,3,2:T(8,128)(2,1)S(1)} %copy-done.8, bf16[16,64,8,1,7,2]{0,4,5,2,1,3:T(8,128)(2,1)} %slice.9, ...), kind=kOutput, calls=%fused_computation.30 | convolution fusion | flops 241065984 | bytes 4975688 | tf_op jit(solution)/shard_map/conv_general_dilated | solution.py:11
  136.4 2.6 copy.64
  139.0 0.4 slice.10
  139.4 1.4 copy.66
  140.8 1.0 fusion.48
  141.8 0.4 copy-done.1
  142.3 0.9 copy.80
  143.2 1.7 slice.16
  144.9 12.4 %fusion.9 = f32[64,32,3,3,3]{0,1,4,3,2:T(8,128)} fusion(bf16[32,4,1,64,32]{4,0,3,1,2:T(8,128)(2,1)} %slice.16, bf16[1,64,16,2,32]{1,4,3,2,0:T(8,128)(2,1)S(1)} %bitcast.60), kind=kOutput, calls=%fused_computation.16 | convolution fusion | flops 91443200 | bytes 876544 | tf_op jit(solution)/shard_map/conv_general_dilated | solution.py:22
  157.3 3.9 add_multiply_fusion
  161.2 4.9 %copy.77 = f32[32,4,8,9,32]{4,0,3,2,1:T(8,128)} copy(f32[32,4,8,9,32]{4,2,3,1,0:T(8,128)S(1)} %add_multiply_fusion) | data formatting | bytes 2359296 | tf_op jit(solution)/shard_map/mul | solution.py:48
  166.1 35.1 %copy.78 = bf16[1,16,64,8,128]{1,0,4,3,2:T(2,128)(2,1)} copy(bf16[1,16,64,8,128]{4,3,1,2,0:T(8,128)(2,1)S(1)} %bitcast.49) | data formatting | bytes 4194304 | tf_op jit(solution)/shard_map/reshape | solution.py:54
  201.2 4.5 %fusion.8 = bf16[32,4,1,64,32]{4,0,3,1,2:T(8,128)(2,1)S(1)} fusion(f32[32,4,1,72,32]{4,0,3,1,2:T(8,128)} %bitcast.52, f32[32,4,1,80,32]{4,0,3,1,2:T(8,128)} %bitcast.51), kind=kLoop, calls=%fused_computation.15 | loop fusion | flops 524288 | bytes 2621440 | tf_op jit(solution)/shard_map/convert_element_type | solution.py:67
  205.7 89.5 %fusion.11 = f32[32,16,3,3,3]{0,1,4,3,2:T(8,128)S(1)} fusion(bf16[1,16,64,8,128]{1,0,4,3,2:T(2,128)(2,1)} %copy.78, bf16[32,4,1,64,32]{4,0,3,1,2:T(8,128)(2,1)S(1)} %fusion.8), kind=kOutput, calls=%fused_computation.18 | convolution fusion | flops 204385280 | bytes 2676736 | tf_op jit(solution)/shard_map/conv_general_dilated | solution.py:22
  295.3 1.8 fusion.26
  297.1 0.2 copy.69
  297.3 1.1 copy.84
  298.4 79.8 %psum.14 = f32[32,16,3,3,3]{0,1,4,3,2:T(8,128)} all-reduce(f32[32,16,3,3,3]{0,1,4,3,2:T(8,128)S(1)} %fusion.11), channel_id=1, replica_groups=mesh['space'=32,'sample'=8] {'space','sample'}, use_global_device_ids=true, to_apply=%region_0.1 | all-reduce | flops 13824 | bytes 110592 | tf_op jit(solution)/shard_map/psum | solution.py:69
  378.2 28.8 %all-reduce.2.cloned.1.call-done = f32[64,32,3,3,3]{0,1,4,3,2:T(8,128)} async-done(((f32[64,32,3,3,3]{0,1,4,3,2:T(8,128)}), f32[64,32,3,3,3]{0,1,4,3,2:T(8,128)}) %all-reduce.2.cloned.1.call-update) | async-done | bytes 221200 | tf_op jit(solution)/shard_map/psum | solution.py:69
  407.0 1.8 copy.101
  (22 shorter events, 0.3 us)
Async XLA Ops:
  7.2 13.7 %copy-start = (bf16[64,32,3,3,3]{0,1,4,3,2:T(8,128)(2,1)S(1)}, bf16[64,32,3,3,3]{0,1,4,3,2:T(8,128)(2,1)}, u32[]{:S(2)}) copy-start(bf16[64,32,3,3,3]{0,1,4,3,2:T(8,128)(2,1)} %param.6) | copy-start | bytes 331780
  7.2 13.7 %copy-start.6 = (pred[8,10]{0,1:T(8,128)(4,1)S(1)}, pred[8,10]{0,1:T(8,128)(4,1)}, u32[]{:S(2)}) copy-start(pred[8,10]{0,1:T(8,128)(4,1)} %constant.19) | copy-start | bytes 244
  7.2 60.5 %all-to-all-start = ((bf16[32,16,2,1024]{3,2,1,0:T(2,128)(2,1)}), bf16[32,16,2,1024]{3,2,1,0:T(2,128)(2,1)S(1)}, u32[]{:S(2)}, u32[]{:S(2)}) async-start(bf16[32,16,2,1024]{3,2,1,0:T(2,128)(2,1)} %param.4), calls=%async_computation | async-start | bytes 4194304 | tf_op jit(solution)/shard_map/all_to_all | solution.py:53
  19.2 387.8 %all-reduce.2.cloned.1.call-start = ((), (), s32[]{:S(2)}) async-start(), calls=%async_computation.1 | async-start | bytes 884736 | tf_op jit(solution)/shard_map/psum | solution.py:69
  79.9 36.3 %copy-start.7 = (pred[8,9]{0,1:T(8,128)(4,1)S(1)}, pred[8,9]{0,1:T(8,128)(4,1)}, u32[]{:S(2)}) copy-start(pred[8,9]{0,1:T(8,128)(4,1)} %constant.17) | copy-start | bytes 220
  79.9 36.3 %copy-start.8 = (bf16[32,16,3,3,3]{0,1,4,3,2:T(8,128)(2,1)S(1)}, bf16[32,16,3,3,3]{0,1,4,3,2:T(8,128)(2,1)}, u32[]{:S(2)}) copy-start(bf16[32,16,3,3,3]{0,1,4,3,2:T(8,128)(2,1)} %param.5) | copy-start | bytes 82948
  139.0 3.3 copy-start.3
  140.8 1.5 copy-start.1
  205.7 89.6 %copy-start.2 = (bf16[32,4,1,8,8,32]{5,3,4,1,0,2:T(8,128)(2,1)S(1)}, bf16[32,4,1,8,8,32]{5,3,4,1,0,2:T(8,128)(2,1)}, u32[]{:S(2)}) copy-start(bf16[32,4,1,8,8,32]{5,3,4,1,0,2:T(8,128)(2,1)} %copy-done.1) | copy-start | bytes 1572868
  205.7 89.6 %copy-start.4 = (bf16[32,4,1,7,1,32]{5,3,4,1,0,2:T(8,128)(2,1)S(1)}, bf16[32,4,1,7,1,32]{5,3,4,1,0,2:T(8,128)(2,1)}, u32[]{:S(2)}) copy-start(bf16[32,4,1,7,1,32]{5,3,4,1,0,2:T(8,128)(2,1)} %get-tuple-element.14) | copy-start | bytes 172036
  205.7 89.6 %copy-start.5 = (bf16[32,4,1,7,1,32]{5,3,4,1,0,2:T(8,128)(2,1)S(1)}, bf16[32,4,1,7,1,32]{5,3,4,1,0,2:T(8,128)(2,1)}, u32[]{:S(2)}) copy-start(bf16[32,4,1,7,1,32]{5,3,4,1,0,2:T(8,128)(2,1)} %get-tuple-element.15) | copy-start | bytes 172036
Sparse Core Ops, SparseCore 0:
  157.4 249.5 all-reduce.1
where the time goes:
time: 422 us; the launch traced here: 416 us
  matrix products  126 us (30%)
  local copies, waits for them, and re-layouts  107 us (25%)
  blocking collectives  79.8 us (19%)
  waiting for transfers between devices  67.7 us (16%)
  between operations  14.5 us (3%)
  starting transfers between devices  12 us (3%)
  other arithmetic  8.48 us (2%)
    conv_general_dilated x2, matrix products, kernel_grad(): lax.conv_general_dilated(field, cotangent, (1, 1, 1), (depth_pad, (1, 0),...  102 us
    psum x1, blocking collectives, body(): lax.psum((first_grad, second_grad), ('space', 'sample'))  79.8 us
    reshape x2, local copies, waits for them, and re-layouts, body(): whole_input.reshape(whole_input.shape[0], channels_in, whole_input.shape[...  40.7 us
    all_to_all x1, waiting for transfers between devices, body(): lax.all_to_all(crops, 'space', split_axis=0, concat_axis=2, tiled=True)  39 us
    conv_general_dilated x2, local copies, waits for them, and re-layouts, forward_conv(): lax.conv_general_dilated(field, kernel, (2, 2, 2), (depth_pad, (1, 0), (1...  36.3 us
    psum x1, waiting for transfers between devices, body(): lax.psum((first_grad, second_grad), ('space', 'sample'))  28.8 us
    conv_general_dilated x2, matrix products, forward_conv(): lax.conv_general_dilated(field, kernel, (2, 2, 2), (depth_pad, (1, 0), (1...  22 us
    all_to_all x1, starting transfers between devices, body(): lax.all_to_all(crops, 'space', split_axis=0, concat_axis=2, tiled=True)  12 us
  transfers between devices with their start and end apart: 2, of which 2 were waited for; matrix products, arithmetic and copies ran while one was open for 36% of the time, Pallas kernels for 0%

commit v1 on v0

--- a/solution.py
+++ b/solution.py
@@ -66,7 +66,10 @@
     act_grad = input_grad(cotangent, second_kernel).astype(jnp.bfloat16)
     pre_grad = (act_grad.astype(jnp.float32) * silu_slope(first_pre)).astype(jnp.bfloat16)
     first_grad = kernel_grad(whole_input, pre_grad, (1, 0))
-    first_grad, second_grad = lax.psum((first_grad, second_grad), ("space", "sample"))
+    flat = jnp.concatenate([first_grad.reshape(-1), second_grad.reshape(-1)])
+    flat = lax.psum(flat, ("space", "sample"))
+    first_grad = flat[: first_grad.size].reshape(first_grad.shape)
+    second_grad = flat[first_grad.size :].reshape(second_grad.shape)
     return (features_out, first_grad, second_grad)
 
 

time: 422 us -> 607 us (1.44)
  waiting for transfers between devices: 67.7 us -> 278 us
  blocking collectives: 79.8 us -> 0 us
  local copies, waits for them, and re-layouts: 107 us -> 160 us
    psum x1, waiting for transfers between devices: 28.8 us -> 239 us  [body(): flat = lax.psum(flat, ('space', 'sample'))]
    psum x1 -> x0, blocking collectives: 79.8 us -> none  [body(): lax.psum((first_grad, second_grad), ('space', 'sample'))]
    reshape x0 -> x4, local copies, waits for them, and re-layouts: none -> 22.9 us  [the longest x2 13 us: body(): flat = jnp.concatenate([first_grad.reshape(-1), second_grad.reshape(-1)])]
    conv_general_dilated x0 -> x2, local copies, waits for them, and re-layouts: none -> 16.7 us  [kernel_grad(): lax.conv_general_dilated(field, cotangent, (1, 1, 1), (depth_pad, (1, 0),...]
    unnamed x24 -> x23, local copies, waits for them, and re-layouts: 10.7 us -> 22.7 us
  transfers between devices with their start and end apart: 2 -> 2, of which waited for: 2 -> 2; matrix products, arithmetic and copies ran while one was open for 36% -> 2% of each run, Pallas kernels for 0% -> 0%
where the time goes in v1:
time: 607 us; the launch traced here: 600 us
  waiting for transfers between devices  278 us (46%)
  local copies, waits for them, and re-layouts  160 us (26%)
  matrix products  128 us (21%)
  between operations  14.4 us (2%)
  starting transfers between devices  12.1 us (2%)
  other arithmetic  7.78 us (1%)
    psum x1, waiting for transfers between devices, body(): flat = lax.psum(flat, ('space', 'sample'))  239 us
    conv_general_dilated x2, matrix products, kernel_grad(): lax.conv_general_dilated(field, cotangent, (1, 1, 1), (depth_pad, (1, 0),...  102 us
    reshape x2, local copies, waits for them, and re-layouts, body(): whole_input.reshape(whole_input.shape[0], channels_in, whole_input.shape[...  40.5 us
    all_to_all x1, waiting for transfers between devices, body(): lax.all_to_all(crops, 'space', split_axis=0, concat_axis=2, tiled=True)  38.9 us
    conv_general_dilated x2, local copies, waits for them, and re-layouts, forward_conv(): lax.conv_general_dilated(field, kernel, (2, 2, 2), (depth_pad, (1, 0), (1...  36.3 us
    conv_general_dilated x2, matrix products, forward_conv(): lax.conv_general_dilated(field, kernel, (2, 2, 2), (depth_pad, (1, 0), (1...  23.7 us
    unnamed x23, local copies, waits for them, and re-layouts  22.7 us
    conv_general_dilated x2, local copies, waits for them, and re-layouts, kernel_grad(): lax.conv_general_dilated(field, cotangent, (1, 1, 1), (depth_pad, (1, 0),...  16.7 us
  transfers between devices with their start and end apart: 2, of which 2 were waited for; matrix products, arithmetic and copies ran while one was open for 2% of the time, Pallas kernels for 0%

profile of v1, /device:TPU:1, one launch (start us, length us, event | category | flops | bytes accessed | tf_op | source)
XLA Modules:
  0.0 600.1 jit_solution(7680147417381081335)
XLA Ops:
  7.2 12.0 %all-to-all-start = ((bf16[32,16,2,1024]{3,2,1,0:T(2,128)(2,1)}), bf16[32,16,2,1024]{3,2,1,0:T(2,128)(2,1)S(1)}, u32[]{:S(2)}, u32[]{:S(2)}) async-start(bf16[32,16,2,1024]{3,2,1,0:T(2,128)(2,1)} %param.4), calls=%async_computation | async-start | bytes 4194304 | tf_op jit(solution)/shard_map/all_to_all | solution.py:53
  19.3 1.2 copy.80
  20.9 2.5 fusion.19
  23.3 5.4 copy.84
  28.7 38.9 %all-to-all-done = bf16[32,16,2,1024]{3,2,1,0:T(2,128)(2,1)S(1)} async-done(((bf16[32,16,2,1024]{3,2,1,0:T(2,128)(2,1)}), bf16[32,16,2,1024]{3,2,1,0:T(2,128)(2,1)S(1)}, u32[]{:S(2)}, u32[]{:S(2)}) %all-to-all-start) | async-done | bytes 2097184 | tf_op jit(solution)/shard_map/all_to_all | solution.py:53
  69.0 4.9 copy.102
  73.9 5.6 pad.clone
  79.5 32.4 %copy.71 = bf16[16,64,8,1,8,18]{0,4,5,2,1,3:T(8,128)(2,1)} copy(bf16[16,64,8,1,8,18]{1,2,5,4,0,3:T(8,128)(2,1)} %bitcast.50) | data formatting | bytes 4718592 | tf_op jit(solution)/shard_map/conv_general_dilated | solution.py:11
  111.9 3.9 slice.33
  115.8 20.2 %broadcast_select_fusion = (bf16[32,4,8,9,32]{4,2,3,1,0:T(8,128)(2,1)}, bf16[32,4,8,9,32]{4,2,3,1,0:T(8,128)(2,1)}, f32[32,4,8,9,32]{4,2,3,1,0:T(8,128)}) fusion(pred[8,9]{0,1:T(8,128)(4,1)S(1)} %copy-done.4, bf16[32,16,3,3,3]{0,1,4,3,2:T(8,128)(2,1)S(1)} %copy-done.5, bf16[16,64,8,1,7,2]{0,4,5,2,1,3:T(8,128)(2,1)} %slice.33, ...), kind=kOutput, calls=%fused_computation.30 | convolution fusion | flops 241065984 | bytes 4975688 | tf_op jit(solution)/shard_map/conv_general_dilated | solution.py:11
  136.0 2.6 copy.72
  139.1 1.4 copy.74
  140.4 1.0 fusion.48
  142.8 1.8 slice.40
  144.6 1.6 add_multiply_fusion
  146.2 4.8 copy.85
  151.0 11.8 %fusion.9 = f32[64,32,3,3,3]{0,1,4,3,2:T(8,128)S(1)} fusion(bf16[32,4,1,64,32]{4,0,3,1,2:T(8,128)(2,1)} %slice.40, bf16[1,64,16,2,32]{1,4,3,2,0:T(8,128)(2,1)S(1)} %bitcast.62), kind=kOutput, calls=%fused_computation.16 | convolution fusion | flops 91443200 | bytes 876544 | tf_op jit(solution)/shard_map/conv_general_dilated | solution.py:22
  162.9 12.3 %copy.93 = f32[64,32,3,3,3]{4,3,2,1,0:T(4,128)} copy(f32[64,32,3,3,3]{0,1,4,3,2:T(8,128)S(1)} %fusion.9) | data formatting | bytes 442368 | tf_op jit(solution)/shard_map/conv_general_dilated | solution.py:22
  175.2 11.0 %reshape.48 = f32[55296]{0:T(1024)} reshape(f32[64,32,3,3,3]{4,3,2,1,0:T(4,128)} %copy.93) | data formatting | bytes 442368 | tf_op jit(solution)/shard_map/reshape | solution.py:69
  186.1 34.9 %copy.86 = bf16[1,16,64,8,128]{1,0,4,3,2:T(2,128)(2,1)} copy(bf16[1,16,64,8,128]{4,3,1,2,0:T(8,128)(2,1)S(1)} %bitcast.49) | data formatting | bytes 4194304 | tf_op jit(solution)/shard_map/reshape | solution.py:54
  221.0 4.5 fusion.8
  225.5 89.8 %fusion.11 = f32[32,16,3,3,3]{0,1,4,3,2:T(8,128)} fusion(bf16[1,16,64,8,128]{1,0,4,3,2:T(2,128)(2,1)} %copy.86, bf16[32,4,1,64,32]{4,0,3,1,2:T(8,128)(2,1)S(1)} %fusion.8), kind=kOutput, calls=%fused_computation.18 | convolution fusion | flops 204385280 | bytes 2676736 | tf_op jit(solution)/shard_map/conv_general_dilated | solution.py:22
  315.3 4.4 copy.88
  319.7 2.0 reshape.47
  321.7 1.7 pad_maximum_fusion
  323.4 3.5 fusion.26
  327.1 1.1 copy.94
  328.1 239.1 %all-reduce.2.cloned.1.call-done = f32[69120]{0:T(1024)} async-done(((f32[69120]{0:T(1024)}), f32[69120]{0:T(1024)}) %all-reduce.2.cloned.1.call-update) | async-done | bytes 276496 | tf_op jit(solution)/shard_map/psum | solution.py:70
  568.1 1.6 reshape.49
  569.6 2.5 copy.95
  573.1 8.3 %reshape.50 = f32[64,32,3,3,3]{4,3,2,1,0:T(4,128)} reshape(f32[55296]{0:T(1024)S(1)} %slice.42) | data formatting | bytes 442368 | tf_op jit(solution)/shard_map/reshape | solution.py:72
  581.4 11.7 %copy.96 = f32[64,32,3,3,3]{0,1,4,3,2:T(8,128)} copy(f32[64,32,3,3,3]{4,3,2,1,0:T(4,128)} %reshape.50) | data formatting | bytes 442368
  (30 shorter events, 5.4 us)
Async XLA Ops:
  7.2 13.7 %copy-start = (bf16[64,32,3,3,3]{0,1,4,3,2:T(8,128)(2,1)S(1)}, bf16[64,32,3,3,3]{0,1,4,3,2:T(8,128)(2,1)}, u32[]{:S(2)}) copy-start(bf16[64,32,3,3,3]{0,1,4,3,2:T(8,128)(2,1)} %param.6) | copy-start | bytes 331780
  7.2 13.7 %copy-start.3 = (pred[8,10]{0,1:T(8,128)(4,1)S(1)}, pred[8,10]{0,1:T(8,128)(4,1)}, u32[]{:S(2)}) copy-start(pred[8,10]{0,1:T(8,128)(4,1)} %constant.19) | copy-start | bytes 244
  7.2 60.5 %all-to-all-start = ((bf16[32,16,2,1024]{3,2,1,0:T(2,128)(2,1)}), bf16[32,16,2,1024]{3,2,1,0:T(2,128)(2,1)S(1)}, u32[]{:S(2)}, u32[]{:S(2)}) async-start(bf16[32,16,2,1024]{3,2,1,0:T(2,128)(2,1)} %param.4), calls=%async_computation | async-start | bytes 4194304 | tf_op jit(solution)/shard_map/all_to_all | solution.py:53
  19.2 548.0 %all-reduce.2.cloned.1.call-start = ((), (), s32[]{:S(2)}) async-start(), calls=%async_computation.1 | async-start | bytes 557056 | tf_op jit(solution)/shard_map/psum | solution.py:70
  79.5 36.3 %copy-start.4 = (pred[8,9]{0,1:T(8,128)(4,1)S(1)}, pred[8,9]{0,1:T(8,128)(4,1)}, u32[]{:S(2)}) copy-start(pred[8,9]{0,1:T(8,128)(4,1)} %constant.17) | copy-start | bytes 220
  79.5 36.3 %copy-start.5 = (bf16[32,16,3,3,3]{0,1,4,3,2:T(8,128)(2,1)S(1)}, bf16[32,16,3,3,3]{0,1,4,3,2:T(8,128)(2,1)}, u32[]{:S(2)}) copy-start(bf16[32,16,3,3,3]{0,1,4,3,2:T(8,128)(2,1)} %param.5) | copy-start | bytes 82948
  138.6 3.3 copy-start.2
  140.4 1.5 copy-start.1
  141.9 2.7 slice-start
  141.9 2.7 slice-start.1
Sparse Core Ops, SparseCore 0:
  323.5 243.6 all-reduce.1

commit v2 on v0

v2 whole, which is shorter than its diff:
```python
import numpy as np

import jax
import jax.numpy as jnp
from jax import lax
from jax.experimental import pallas as pl
from jax.experimental.pallas import tpu as pltpu
from jax.sharding import PartitionSpec as P

HEIGHT = 8
WIDTH = 128

NT = (((1,), (1,)), ((), ()))


def selection_tables(c0_w, c1_h, c1_w):
    t1 = np.zeros((c0_w, 3 * 128), np.float32)
    for c in range(3):
        for pw in range(c0_w // 2):
            w = 2 * pw + c - 1
            if 0 <= w < c0_w:
                t1[w, c * 128 + pw] = 1.0
    q_h, q_w = c1_h // 2, c1_w // 2
    sel2 = np.zeros((c1_h * c1_w, 9 * 128), np.float32)
    up = np.zeros((q_h * q_w, 9 * c1_h * c1_w), np.float32)
    for b in range(3):
        for c in range(3):
            bc = b * 3 + c
            for qh in range(q_h):
                for qw in range(q_w):
                    h2, w2 = 2 * qh + b - 1, 2 * qw + c - 1
                    if 0 <= h2 < c1_h and 0 <= w2 < c1_w:
                        sel2[h2 * c1_w + w2, bc * 128 + qh * q_w + qw] = 1.0
                        up[qh * q_w + qw, bc * c1_h * c1_w + h2 * c1_w + w2] = 1.0
    return t1, sel2, up


def conv_kernel(x_ref, ogn_ref, ogq_ref, w1_ref, w2_ref, w2t_ref, t1_ref, sel2_ref, up_ref,
                feat_ref, fg_ref, sg_ref,
                q1_ref, s_ref, fp_ref, a2_ref, q2_ref, s2_ref, v_ref):
    depth, c0, cells = x_ref.shape
    n_h = cells // 128
    c1 = w1_ref.shape[0]
    c2 = w2_ref.shape[0]
    planes1 = depth // 2
    plane1 = s_ref.shape[2]
    planes2 = planes1 // 2
    plane2 = ogq_ref.shape[1]

    q1_ref[0] = jnp.zeros(q1_ref.shape[1:], q1_ref.dtype)
    for h in range(n_h):
        xh = x_ref[:, :, h * 128:(h + 1) * 128].reshape(depth * c0, 128)
        qh = jnp.dot(xh, t1_ref[...], preferred_element_type=jnp.float32)
        q1_ref[pl.ds(1, depth), :, h * 384:(h + 1) * 384] = qh.astype(q1_ref.dtype).reshape(depth, c0, 384)

    a2_ref[0] = jnp.zeros(a2_ref.shape[1:], a2_ref.dtype)

    def build_plane(pd, carry):
        for a in range(3):
            for b in range(3):
                for c in range(3):
                    r0 = ((a * 3 + b) * 3 + c) * c0
                    for m in range(plane1 // 128):
                        h_lo, h_hi = 4 * m + b - 1, 4 * m + b + 1
                        hi = q1_ref[2 * pd + a, :, pl.ds((h_hi * 3 + c) * 128, 128)].astype(jnp.float32)
                        val = pltpu.roll(hi, 64, 1)
                        if h_lo >= 0:
                            val = val + q1_ref[2 * pd + a, :, pl.ds((h_lo * 3 + c) * 128, 128)].astype(jnp.float32)
                        s_ref[pd, pl.ds(r0, c0), pl.ds(m * 128, 128)] = val.astype(s_ref.dtype)
        pre = jnp.dot(w1_ref[...], s_ref[pd], preferred_element_type=jnp.float32)
        fp_ref[pd] = pre
        sig = 1.0 / (1.0 + jnp.exp(-pre))
        a2_ref[pd + 1] = (pre * sig).astype(a2_ref.dtype)
        return carry

    lax.fori_loop(0, planes1, build_plane, 0)

    a2 = a2_ref[...].reshape((planes1 + 1) * c1, plane1)
    for bc in range(9):
        q2 = jnp.dot(a2, sel2_ref[:, bc * 128:(bc + 1) * 128], preferred_element_type=jnp.float32)
        q2_ref[:, :, bc * 128:(bc + 1) * 128] = q2.reshape(planes1 + 1, c1, 128)

    sg_ref[...] = jnp.zeros(sg_ref.shape, sg_ref.dtype)
    for n in range(planes2 // 2):
        for a in range(3):
            for bc in range(9):
                r0 = (a * 9 + bc) * c1
                lo = q2_ref[4 * n + a, :, bc * 128:(bc + 1) * 128]
                hi = q2_ref[4 * n + a + 2, :, bc * 128:(bc + 1) * 128]
                s2_ref[n, r0:r0 + c1, :] = (lo + pltpu.roll(hi, 64, 1)).astype(s2_ref.dtype)
        feat = jnp.dot(w2_ref[...], s2_ref[n], preferred_element_type=jnp.float32)
        feat_ref[:, n * 128:(n + 1) * 128] = feat.astype(feat_ref.dtype)
        sg_ref[...] += lax.dot_general(ogn_ref[:, n * 128:(n + 1) * 128], s2_ref[n], NT,
                                       preferred_element_type=jnp.float32)

    v_ref[planes2] = jnp.zeros(v_ref.shape[1:], v_ref.dtype)
    span = up_ref.shape[1] // 9
    for bc in range(9):
        u = jnp.dot(ogq_ref[...], up_ref[:, bc * span:(bc + 1) * span], preferred_element_type=jnp.float32)
        v_ref[pl.ds(0, planes2), bc] = u.astype(v_ref.dtype).reshape(planes2, c2, span)

    fg_ref[...] = jnp.zeros(fg_ref.shape, fg_ref.dtype)

    def back_plane(q, carry):
        vq = v_ref[q].reshape(9 * c2, span)
        vq1 = v_ref[q + 1].reshape(9 * c2, span)
        even = jnp.dot(w2t_ref[1], vq, preferred_element_type=jnp.float32)
        odd = (jnp.dot(w2t_ref[2], vq, preferred_element_type=jnp.float32)
               + jnp.dot(w2t_ref[0], vq1, preferred_element_type=jnp.float32))
        for k, act in ((0, even), (1, odd)):
            d2 = 2 * q + k
            pre = fp_ref[d2]
            sig = 1.0 / (1.0 + jnp.exp(-pre))
            slope = sig * (1.0 + pre * (1.0 - sig))
            pg = (act.astype(jnp.bfloat16).astype(jnp.float32) * slope).astype(jnp.bfloat16)
            fg_ref[...] += lax.dot_general(pg, s_ref[d2], NT, preferred_element_type=jnp.float32)
        return carry

    lax.fori_loop(0, planes2, back_plane, 0)


def per_sample(x, ogn, ogq, w1, w2, w2t, t1, sel2, up):
    depth, c0, cells = x.shape
    c1, c2 = w1.shape[0], w2.shape[0]
    planes1, planes2 = depth // 2, depth // 4
    plane1 = (HEIGHT // 2) * (WIDTH // 2)
    plane2 = ogq.shape[1]
    vmem = pltpu.VMEM
    return pl.pallas_call(
        conv_kernel,
        out_shape=(
            jax.ShapeDtypeStruct((c2, planes2 * plane2), jnp.bfloat16),
            jax.ShapeDtypeStruct((c1, 27 * c0), jnp.float32),
            jax.ShapeDtypeStruct((c2, 27 * c1), jnp.float32),
        ),
        in_specs=[pl.BlockSpec(memory_space=vmem)] * 9,
        out_specs=[pl.BlockSpec(memory_space=vmem)] * 3,
        scratch_shapes=[
            vmem((depth + 1, c0, (cells // 128) * 384), jnp.bfloat16),
            vmem((planes1, 27 * c0, plane1), jnp.bfloat16),
            vmem((planes1, c1, plane1), jnp.float32),
            vmem((planes1 + 1, c1, plane1), jnp.bfloat16),
            vmem((planes1 + 1, c1, 9 * 128), jnp.float32),
            vmem((planes2 // 2, 27 * c1, 128), jnp.bfloat16),
            vmem((planes2 + 1, 9, c2, plane1), jnp.bfloat16),
        ],
        compiler_params=pltpu.CompilerParams(vmem_limit_bytes=60 * 1024 * 1024),
    )(x, ogn, ogq, w1, w2, w2t, t1, sel2, up)


def body(crops, first_kernel, second_kernel, out_grad):
    local_samples, channels_in, planes, flat_cells = crops.shape
    whole_input = lax.all_to_all(crops, "space", split_axis=0, concat_axis=2, tiled=True)
    x = whole_input[0].transpose(1, 0, 2)
    c1, c2 = first_kernel.shape[0], second_kernel.shape[0]
    og = out_grad[0]
    ogn = og.reshape(c2, -1)
    ogq = og.transpose(1, 0, 2).reshape(-1, og.shape[2])
    w1 = first_kernel.transpose(0, 2, 3, 4, 1).reshape(c1, -1)
    w2 = second_kernel.transpose(0, 2, 3, 4, 1).reshape(c2, -1)
    w2t = second_kernel.transpose(2, 1, 3, 4, 0).reshape(3, c1, -1)
    t1, sel2, up = selection_tables(WIDTH, HEIGHT // 2, WIDTH // 2)
    feat, fg, sg = per_sample(
        x, ogn, ogq, w1, w2, w2t,
        jnp.asarray(t1, jnp.bfloat16), jnp.asarray(sel2, jnp.bfloat16), jnp.asarray(up, jnp.bfloat16),
    )
    features_out = feat.reshape(out_grad.shape)
    first_grad = fg.reshape(c1, 3, 3, 3, channels_in).transpose(0, 4, 1, 2, 3)
    second_grad = sg.reshape(c2, 3, 3, 3, c1).transpose(0, 4, 1, 2, 3)
    first_grad, second_grad = lax.psum((first_grad, second_grad), ("space", "sample"))
    return (features_out, first_grad, second_grad)


def solution(mesh):
    placed = (P("sample", None, "space", None), P(), P(), P(("sample", "space"), None, None, None))
    return jax.shard_map(
        body,
        mesh=mesh,
        in_specs=placed,
        out_specs=(P(("sample", "space"), None, None, None), P(), P()),
        check_vma=False,
    )
```

time: 422 us -> 355 us (0.84); the launches traced: 416 us -> 355 us
  waiting for transfers between devices: 67.7 us -> 211 us
  matrix products: 126 us -> 0 us
  local copies, waits for them, and re-layouts: 107 us -> 12.7 us
  Pallas kernels: 0 us -> 24.7 us
  other arithmetic: 8.48 us -> 0 us
    psum x1, waiting for transfers between devices: 28.8 us -> 167 us  [body(): lax.psum((first_grad, second_grad), ('space', 'sample'))]
    conv_general_dilated x5 -> x0, matrix products: 126 us -> none  [the longest x2 102 us: kernel_grad(): lax.conv_general_dilated(field, cotangent, (1, 1, 1), (depth_pad, (1, 0),...]
    reshape x3 -> x4, local copies, waits for them, and re-layouts: 40.7 us -> 4.19 us  [the longest x1 1.83 us: body(): features_out = feat.reshape(out_grad.shape)]
    conv_general_dilated x4 -> x0, local copies, waits for them, and re-layouts: 36.4 us -> none  [the longest x2 36.3 us: forward_conv(): lax.conv_general_dilated(field, kernel, (2, 2, 2), (depth_pad, (1, 0), (1...]
    pallas_call x0 -> x1, Pallas kernels: none -> 24.7 us  [per_sample(): pl.pallas_call(conv_kernel, out_shape=(jax.ShapeDtypeStruct((c2, planes2...]
    convert_element_type x8 -> x0, local copies, waits for them, and re-layouts: 13.6 us -> none  [the longest x6 7.98 us: body(): act_whole = jax.nn.silu(first_pre).astype(jnp.bfloat16)]
    unnamed x24 -> x7, local copies, waits for them, and re-layouts: 10.7 us -> 1.82 us
    all_to_all x1, waiting for transfers between devices: 39 us -> 44.3 us  [body(): lax.all_to_all(crops, 'space', split_axis=0, concat_axis=2, tiled=True)]
  transfers between devices with their start and end apart: 2 -> 2, of which waited for: 2 -> 2; matrix products, arithmetic and copies ran while one was open for 36% -> 2% of each run, Pallas kernels for 0% -> 0%
where the time goes in v2:
time: 355 us
  waiting for transfers between devices  211 us (59%)
  blocking collectives  79.8 us (22%)
  Pallas kernels  24.7 us (7%)
  between operations  14.1 us (4%)
  local copies, waits for them, and re-layouts  12.7 us (4%)
  starting transfers between devices  12 us (3%)
    psum x1, waiting for transfers between devices, body(): lax.psum((first_grad, second_grad), ('space', 'sample'))  167 us
    psum x1, blocking collectives, body(): lax.psum((first_grad, second_grad), ('space', 'sample'))  79.8 us
    all_to_all x1, waiting for transfers between devices, body(): lax.all_to_all(crops, 'space', split_axis=0, concat_axis=2, tiled=True)  44.3 us
    pallas_call x1, Pallas kernels, per_sample(): pl.pallas_call(conv_kernel, out_shape=(jax.ShapeDtypeStruct((c2, planes2...  24.7 us
    all_to_all x1, starting transfers between devices, body(): lax.all_to_all(crops, 'space', split_axis=0, concat_axis=2, tiled=True)  12 us
  transfers between devices with their start and end apart: 2, of which 2 were waited for; matrix products, arithmetic and copies ran while one was open for 2% of the time, Pallas kernels for 0%

profile of v2, /device:TPU:1, one launch (start us, length us, event | category | flops | bytes accessed | tf_op | source)
XLA Modules:
  0.0 354.6 jit_solution(4090366895347257155)
XLA Ops:
  7.2 0.0 copy-start.2
  7.2 0.0 copy-start.1
  7.2 0.0 copy-start
  7.2 12.0 %all-to-all-start = ((bf16[32,16,2,1024]{3,2,1,0:T(2,128)(2,1)}), bf16[32,16,2,1024]{3,2,1,0:T(2,128)(2,1)S(1)}, u32[]{:S(2)}, u32[]{:S(2)}) async-start(bf16[32,16,2,1024]{3,2,1,0:T(2,128)(2,1)} %param.7), calls=%async_computation | async-start | bytes 4194304 | tf_op jit(solution)/shard_map/all_to_all | solution.py:153
  19.2 0.0 all-reduce.2.cloned.1.call-start
  19.3 0.0 copy-done.2
  19.3 0.7 copy.20.w1_ref
  20.0 0.0 copy-done.1
  20.0 0.8 copy.21.w2_ref
  20.8 0.0 copy-done
  20.8 0.9 reshape_squeeze.3.ogn_ref
  21.6 0.8 copy.18
  22.4 0.2 copy.19
  22.6 0.9 reshape.31.w2t_ref
  23.4 44.3 %all-to-all-done = bf16[32,16,2,1024]{3,2,1,0:T(2,128)(2,1)S(1)} async-done(((bf16[32,16,2,1024]{3,2,1,0:T(2,128)(2,1)}), bf16[32,16,2,1024]{3,2,1,0:T(2,128)(2,1)S(1)}, u32[]{:S(2)}, u32[]{:S(2)}) %all-to-all-start) | async-done | bytes 2097184 | tf_op jit(solution)/shard_map/all_to_all | solution.py:153
  67.7 2.0 copy.17
  69.7 24.7 %shard_map.94 = (bf16[64,1024]{1,0:T(8,128)(2,1)}, f32[32,432]{1,0:T(8,128)}, f32[64,864]{1,0:T(8,128)}) custom-call(bf16[64,16,1024]{2,1,0:T(8,128)(2,1)} %bitcast.25, bf16[64,1024]{1,0:T(8,128)(2,1)} %reshape_squeeze.3.ogn_ref, bf16[1024,64]{1,0:T(8,128)(2,1)} %bitcast.28, bf16[32,432]{1,0:T(8,128)(2,1)} %copy.20.w1_ref, bf16[64,864]{1,0:T(8,128)(2,1)} %copy.21.w2_ref, ...), custom_call_target="tpu_custom_call" | custom-call | tf_op jit(solution)/shard_map/pallas_call | solution.py:129
  94.4 1.9 copy.23
  96.3 0.0 all-reduce.2.cloned.1.call-update
  96.3 1.8 reshape.32
  98.2 1.0 copy.22
  99.1 79.8 %psum.14 = f32[32,16,3,3,3]{0,1,4,3,2:T(8,128)} all-reduce(f32[32,16,3,3,3]{0,1,4,3,2:T(8,128)S(1)} %bitcast.30), channel_id=1, replica_groups=mesh['space'=32,'sample'=8] {'space','sample'}, use_global_device_ids=true, to_apply=%region_0.0 | all-reduce | flops 13824 | bytes 110592 | tf_op jit(solution)/shard_map/psum | solution.py:170
  179.0 167.0 %all-reduce.2.cloned.1.call-done = f32[64,32,3,3,3]{0,1,4,3,2:T(8,128)} async-done(((f32[64,32,3,3,3]{0,1,4,3,2:T(8,128)}), f32[64,32,3,3,3]{0,1,4,3,2:T(8,128)}) %all-reduce.2.cloned.1.call-update) | async-done | bytes 221200 | tf_op jit(solution)/shard_map/psum | solution.py:170
  345.9 1.8 copy.25
Async XLA Ops:
  7.2 12.1 %copy-start.2 = (bf16[32,16,3,3,3]{0,1,4,3,2:T(8,128)(2,1)S(1)}, bf16[32,16,3,3,3]{0,1,4,3,2:T(8,128)(2,1)}, u32[]{:S(2)}) copy-start(bf16[32,16,3,3,3]{0,1,4,3,2:T(8,128)(2,1)} %param.8) | copy-start | bytes 82948
  7.2 12.8 %copy-start.1 = (bf16[64,32,3,3,3]{0,1,4,3,2:T(8,128)(2,1)S(1)}, bf16[64,32,3,3,3]{0,1,4,3,2:T(8,128)(2,1)}, u32[]{:S(2)}) copy-start(bf16[64,32,3,3,3]{0,1,4,3,2:T(8,128)(2,1)} %param.9) | copy-start | bytes 331780
  7.2 13.6 %copy-start = (bf16[1,64,16,64]{3,2,1,0:T(8,128)(2,1)S(1)}, bf16[1,64,16,64]{3,2,1,0:T(8,128)(2,1)}, u32[]{:S(2)}) copy-start(bf16[1,64,16,64]{3,2,1,0:T(8,128)(2,1)} %param.10) | copy-start | bytes 393220
  7.2 60.5 %all-to-all-start = ((bf16[32,16,2,1024]{3,2,1,0:T(2,128)(2,1)}), bf16[32,16,2,1024]{3,2,1,0:T(2,128)(2,1)S(1)}, u32[]{:S(2)}, u32[]{:S(2)}) async-start(bf16[32,16,2,1024]{3,2,1,0:T(2,128)(2,1)} %param.7), calls=%async_computation | async-start | bytes 4194304 | tf_op jit(solution)/shard_map/all_to_all | solution.py:153
  19.2 326.7 %all-reduce.2.cloned.1.call-start = ((), (), s32[]{:S(2)}) async-start(), calls=%async_computation.1 | async-start | bytes 884736 | tf_op jit(solution)/shard_map/psum | solution.py:170
Sparse Core Ops, SparseCore 0:
  96.5 249.4 all-reduce.1

commit v3 on v2

--- a/solution.py
+++ b/solution.py
@@ -1,3 +1,5 @@
+import functools
+
 import numpy as np
 
 import jax
@@ -148,7 +150,65 @@
     )(x, ogn, ogq, w1, w2, w2t, t1, sel2, up)
 
 
-def body(crops, first_kernel, second_kernel, out_grad):
+def partner_steps(axis_sizes):
+    steps = []
+    for axis, size in axis_sizes:
+        bit = 1
+        while bit < size:
+            steps.append((axis, bit))
+            bit *= 2
+    return steps
+
+
+def allreduce_kernel(axis_order, steps, g1_ref, g2_ref, o1_ref, o2_ref, r1_ref, r2_ref, send_sem, recv_sem):
+    me = {axis: lax.axis_index(axis) for axis in axis_order}
+    partners = []
+    for axis, bit in steps:
+        there = dict(me)
+        there[axis] = me[axis] + bit - 2 * bit * ((me[axis] // bit) % 2)
+        partners.append(tuple(there[a] for a in axis_order))
+
+    barrier = pltpu.get_barrier_semaphore()
+    for partner in partners:
+        pl.semaphore_signal(barrier, 1, device_id=partner, device_id_type=pl.DeviceIdType.MESH)
+    pl.semaphore_wait(barrier, len(partners))
+
+    o1_ref[...] = g1_ref[...]
+    o2_ref[...] = g2_ref[...]
+    for s, partner in enumerate(partners):
+        copies = [
+            pltpu.make_async_remote_copy(
+                src_ref=src, dst_ref=dst.at[s], send_sem=send_sem.at[s, k], recv_sem=recv_sem.at[s, k],
+                device_id=partner, device_id_type=pl.DeviceIdType.MESH)
+            for k, (src, dst) in enumerate(((o1_ref, r1_ref), (o2_ref, r2_ref)))
+        ]
+        for copy in copies:
+            copy.start()
+        for copy in copies:
+            copy.wait()
+        o1_ref[...] = o1_ref[...] + r1_ref[s]
+        o2_ref[...] = o2_ref[...] + r2_ref[s]
+
+
+def allreduce(g1, g2, axis_order, axis_sizes):
+    steps = partner_steps(axis_sizes)
+    vmem = pltpu.VMEM
+    return pl.pallas_call(
+        functools.partial(allreduce_kernel, axis_order, steps),
+        out_shape=(jax.ShapeDtypeStruct(g1.shape, g1.dtype), jax.ShapeDtypeStruct(g2.shape, g2.dtype)),
+        in_specs=[pl.BlockSpec(memory_space=vmem)] * 2,
+        out_specs=[pl.BlockSpec(memory_space=vmem)] * 2,
+        scratch_shapes=[
+            vmem((len(steps),) + g1.shape, g1.dtype),
+            vmem((len(steps),) + g2.shape, g2.dtype),
+            pltpu.SemaphoreType.DMA((len(steps), 2)),
+            pltpu.SemaphoreType.DMA((len(steps), 2)),
+        ],
+        compiler_params=pltpu.CompilerParams(collective_id=0, has_side_effects=True),
+    )(g1, g2)
+
+
+def body(axis_order, axis_sizes, crops, first_kernel, second_kernel, out_grad):
     local_samples, channels_in, planes, flat_cells = crops.shape
     whole_input = lax.all_to_all(crops, "space", split_axis=0, concat_axis=2, tiled=True)
     x = whole_input[0].transpose(1, 0, 2)
@@ -165,16 +225,18 @@
         jnp.asarray(t1, jnp.bfloat16), jnp.asarray(sel2, jnp.bfloat16), jnp.asarray(up, jnp.bfloat16),
     )
     features_out = feat.reshape(out_grad.shape)
+    fg, sg = allreduce(fg, sg, axis_order, axis_sizes)
     first_grad = fg.reshape(c1, 3, 3, 3, channels_in).transpose(0, 4, 1, 2, 3)
     second_grad = sg.reshape(c2, 3, 3, 3, c1).transpose(0, 4, 1, 2, 3)
-    first_grad, second_grad = lax.psum((first_grad, second_grad), ("space", "sample"))
     return (features_out, first_grad, second_grad)
 
 
 def solution(mesh):
     placed = (P("sample", None, "space", None), P(), P(), P(("sample", "space"), None, None, None))
+    axis_order = tuple(mesh.axis_names)
+    axis_sizes = [(a, mesh.shape[a]) for a in ("sample", "space")]
     return jax.shard_map(
-        body,
+        functools.partial(body, axis_order, axis_sizes),
         mesh=mesh,
         in_specs=placed,
         out_specs=(P(("sample", "space"), None, None, None), P(), P()),

time: 355 us -> 174 us (0.49)
  the two profiles are of different devices: /device:TPU:1 before, /device:TPU:166 now
where the time goes in v3:
time: 174 us
  Pallas kernels  110 us (63%)
  waiting for transfers between devices  42.4 us (24%)
  local copies, waits for them, and re-layouts  11.5 us (7%)
  starting transfers between devices  9.47 us (5%)
    pallas_call x1, Pallas kernels, allreduce(): pl.pallas_call(functools.partial(allreduce_kernel, axis_order, steps), ou...  85.2 us
    all_to_all x1, waiting for transfers between devices, body(): lax.all_to_all(crops, 'space', split_axis=0, concat_axis=2, tiled=True)  42.4 us
    pallas_call x1, Pallas kernels, per_sample(): pl.pallas_call(conv_kernel, out_shape=(jax.ShapeDtypeStruct((c2, planes2...  24.7 us
    all_to_all x1, starting transfers between devices, body(): lax.all_to_all(crops, 'space', split_axis=0, concat_axis=2, tiled=True)  9.47 us
    pallas_call x2, local copies, waits for them, and re-layouts, allreduce(): pl.pallas_call(functools.partial(allreduce_kernel, axis_order, steps), ou...  3.56 us
  transfers between devices with their start and end apart: 1, of which 1 were waited for; matrix products, arithmetic and copies ran while one was open for 2% of the time, Pallas kernels for 0%

profile of v3, /device:TPU:166, one launch (start us, length us, event | category | flops | bytes accessed | tf_op | source)
XLA Modules:
  0.0 173.9 jit_solution(4839549243117800811)
XLA Ops:
  0.6 0.0 copy-start.2
  0.6 0.0 copy-start.1
  0.7 0.0 copy-start
  0.7 9.5 %all-to-all-start = ((bf16[32,16,2,1024]{3,2,1,0:T(2,128)(2,1)}), bf16[32,16,2,1024]{3,2,1,0:T(2,128)(2,1)S(1)}, u32[]{:S(2)}, u32[]{:S(2)}) async-start(bf16[32,16,2,1024]{3,2,1,0:T(2,128)(2,1)} %param.7), calls=%async_computation | async-start | bytes 4194304 | tf_op jit(solution)/shard_map/all_to_all | solution.py:213
  10.1 0.0 copy-done.2
  10.1 0.7 copy.20.w1_ref
  10.8 0.0 copy-done.1
  10.8 0.8 copy.21.w2_ref
  11.6 0.0 copy-done
  11.6 0.9 reshape_squeeze.3.ogn_ref
  12.5 0.8 copy.18
  13.2 0.2 copy.19
  13.4 0.9 reshape.31.w2t_ref
  14.3 42.4 %all-to-all-done = bf16[32,16,2,1024]{3,2,1,0:T(2,128)(2,1)S(1)} async-done(((bf16[32,16,2,1024]{3,2,1,0:T(2,128)(2,1)}), bf16[32,16,2,1024]{3,2,1,0:T(2,128)(2,1)S(1)}, u32[]{:S(2)}, u32[]{:S(2)}) %all-to-all-start) | async-done | bytes 2097184 | tf_op jit(solution)/shard_map/all_to_all | solution.py:213
  56.6 2.0 %copy.17 = bf16[1,16,32,2,1024]{4,1,3,2,0:T(8,128)(2,1)} copy(bf16[1,16,32,2,1024]{4,3,1,2,0:T(2,128)(2,1)S(1)} %bitcast.26) | data formatting | bytes 4194304 | tf_op jit(solution)/shard_map/all_to_all | solution.py:213
  58.7 24.7 %shard_map.94 = (bf16[64,1024]{1,0:T(8,128)(2,1)}, f32[32,432]{1,0:T(8,128)}, f32[64,864]{1,0:T(8,128)}) custom-call(bf16[64,16,1024]{2,1,0:T(8,128)(2,1)} %bitcast.25, bf16[64,1024]{1,0:T(8,128)(2,1)} %reshape_squeeze.3.ogn_ref, bf16[1024,64]{1,0:T(8,128)(2,1)} %bitcast.27, bf16[32,432]{1,0:T(8,128)(2,1)} %copy.20.w1_ref, bf16[64,864]{1,0:T(8,128)(2,1)} %copy.21.w2_ref, ...), custom_call_target="tpu_custom_call" | custom-call | tf_op jit(solution)/shard_map/pallas_call | solution.py:131
  83.4 1.8 %reshape.32 = bf16[1,64,16,64]{3,2,1,0:T(8,128)(2,1)} reshape(bf16[64,1024]{1,0:T(8,128)(2,1)} %get-tuple-element.8) | data formatting | bytes 262144 | tf_op jit(solution)/shard_map/reshape | solution.py:227
  85.2 85.2 %shard_map.95 = (f32[32,432]{1,0:T(8,128)}, f32[64,864]{1,0:T(8,128)}) custom-call(f32[32,432]{1,0:T(8,128)} %get-tuple-element.9.g1_ref, f32[64,864]{1,0:T(8,128)} %get-tuple-element.10.g2_ref), custom_call_target="tpu_custom_call" | custom-call | tf_op jit(solution)/shard_map/pallas_call | solution.py:196
  170.4 1.7 copy.22
  172.0 1.9 %copy.23 = f32[64,864]{0,1:T(8,128)} copy(f32[64,864]{1,0:T(8,128)} %get-tuple-element.12) | data formatting | bytes 442368 | tf_op jit(solution)/shard_map/pallas_call | solution.py:196
Async XLA Ops:
  0.6 9.5 %copy-start.2 = (bf16[32,16,3,3,3]{0,1,4,3,2:T(8,128)(2,1)S(1)}, bf16[32,16,3,3,3]{0,1,4,3,2:T(8,128)(2,1)}, u32[]{:S(2)}) copy-start(bf16[32,16,3,3,3]{0,1,4,3,2:T(8,128)(2,1)} %param.8) | copy-start | bytes 82948
  0.6 10.2 %copy-start.1 = (bf16[64,32,3,3,3]{0,1,4,3,2:T(8,128)(2,1)S(1)}, bf16[64,32,3,3,3]{0,1,4,3,2:T(8,128)(2,1)}, u32[]{:S(2)}) copy-start(bf16[64,32,3,3,3]{0,1,4,3,2:T(8,128)(2,1)} %param.9) | copy-start | bytes 331780
  0.7 11.0 %copy-start = (bf16[1,64,16,64]{3,2,1,0:T(8,128)(2,1)S(1)}, bf16[1,64,16,64]{3,2,1,0:T(8,128)(2,1)}, u32[]{:S(2)}) copy-start(bf16[1,64,16,64]{3,2,1,0:T(8,128)(2,1)} %param.10) | copy-start | bytes 393220
  0.7 56.0 %all-to-all-start = ((bf16[32,16,2,1024]{3,2,1,0:T(2,128)(2,1)}), bf16[32,16,2,1024]{3,2,1,0:T(2,128)(2,1)S(1)}, u32[]{:S(2)}, u32[]{:S(2)}) async-start(bf16[32,16,2,1024]{3,2,1,0:T(2,128)(2,1)} %param.7), calls=%async_computation | async-start | bytes 4194304 | tf_op jit(solution)/shard_map/all_to_all | solution.py:213

commit v4 on v3

--- a/solution.py
+++ b/solution.py
@@ -150,44 +150,97 @@
     )(x, ogn, ogq, w1, w2, w2t, t1, sel2, up)
 
 
+STEP_ORDER = (("sample", 1), ("space", 4), ("sample", 2), ("space", 1),
+              ("space", 2), ("sample", 4), ("space", 8), ("space", 16))
+
+
 def partner_steps(axis_sizes):
-    steps = []
+    sizes = dict(axis_sizes)
+    steps = [(axis, bit) for axis, bit in STEP_ORDER if bit < sizes[axis]]
     for axis, size in axis_sizes:
         bit = 1
         while bit < size:
-            steps.append((axis, bit))
+            if (axis, bit) not in steps:
+                steps.append((axis, bit))
             bit *= 2
     return steps
 
 
-def allreduce_kernel(axis_order, steps, g1_ref, g2_ref, o1_ref, o2_ref, r1_ref, r2_ref, send_sem, recv_sem):
+def halvings(rows, steps):
+    count = 0
+    while count < len(steps) and rows % (2 ** (count + 1) * 8) == 0:
+        count += 1
+    return count
+
+
+def allreduce_kernel(axis_order, steps, g1_ref, g2_ref, o1_ref, o2_ref, r1_ref, r2_ref, a1_ref, a2_ref,
+                     send_sem, recv_sem):
     me = {axis: lax.axis_index(axis) for axis in axis_order}
-    partners = []
+    partners, bits = [], []
     for axis, bit in steps:
+        mine = (me[axis] // bit) % 2
         there = dict(me)
-        there[axis] = me[axis] + bit - 2 * bit * ((me[axis] // bit) % 2)
+        there[axis] = me[axis] + bit - 2 * bit * mine
         partners.append(tuple(there[a] for a in axis_order))
+        bits.append(mine)
 
     barrier = pltpu.get_barrier_semaphore()
     for partner in partners:
         pl.semaphore_signal(barrier, 1, device_id=partner, device_id_type=pl.DeviceIdType.MESH)
     pl.semaphore_wait(barrier, len(partners))
 
+    accs = (o1_ref, o2_ref)
+    recvs = (r1_ref, r2_ref)
+    gathers = (a1_ref, a2_ref)
     o1_ref[...] = g1_ref[...]
     o2_ref[...] = g2_ref[...]
-    for s, partner in enumerate(partners):
-        copies = [
-            pltpu.make_async_remote_copy(
-                src_ref=src, dst_ref=dst.at[s], send_sem=send_sem.at[s, k], recv_sem=recv_sem.at[s, k],
-                device_id=partner, device_id_type=pl.DeviceIdType.MESH)
-            for k, (src, dst) in enumerate(((o1_ref, r1_ref), (o2_ref, r2_ref)))
-        ]
+    n_steps = len(steps)
+    plans = []
+    for acc in accs:
+        plans.append({"rows": acc.shape[0], "h": halvings(acc.shape[0], steps), "off": 0, "kept": []})
+
+    def remote(src, dst, slot, k, partner):
+        return pltpu.make_async_remote_copy(
+            src_ref=src, dst_ref=dst, send_sem=send_sem.at[slot, k], recv_sem=recv_sem.at[slot, k],
+            device_id=partner, device_id_type=pl.DeviceIdType.MESH)
+
+    for s in range(n_steps):
+        copies, adds = [], []
+        for k, (acc, recv, plan) in enumerate(zip(accs, recvs, plans)):
+            if s < plan["h"]:
+                half = plan["rows"] // 2
+                keep = pl.multiple_of(plan["off"] + bits[s] * half, 8)
+                give = pl.multiple_of(plan["off"] + (1 - bits[s]) * half, 8)
+                copies.append(remote(acc.at[pl.ds(give, half)], recv.at[s, pl.ds(0, half)], s, k, partners[s]))
+                adds.append((acc, recv, s, keep, half))
+                plan["kept"].append((s, keep, give, half))
+                plan["off"], plan["rows"] = keep, half
+            else:
+                rows = plan["rows"]
+                off = plan["off"]
+                copies.append(remote(acc.at[pl.ds(off, rows)], recv.at[s, pl.ds(0, rows)], s, k, partners[s]))
+                adds.append((acc, recv, s, off, rows))
         for copy in copies:
             copy.start()
         for copy in copies:
             copy.wait()
-        o1_ref[...] = o1_ref[...] + r1_ref[s]
-        o2_ref[...] = o2_ref[...] + r2_ref[s]
+        for acc, recv, slot, off, rows in adds:
+            acc[pl.ds(off, rows)] = acc[pl.ds(off, rows)] + recv[slot, pl.ds(0, rows)]
+
+    for s in reversed(range(n_steps)):
+        copies, places = [], []
+        for k, (acc, gather, plan) in enumerate(zip(accs, gathers, plans)):
+            for step, keep, give, half in plan["kept"]:
+                if step == s:
+                    copies.append(remote(acc.at[pl.ds(keep, half)], gather.at[s, pl.ds(0, half)],
+                                         n_steps + s, k, partners[s]))
+                    places.append((acc, gather, give, half))
+        for copy in copies:
+            copy.start()
+        for copy in copies:
+            copy.wait()
+        for acc, gather, give, half in places:
+            acc[pl.ds(give, half)] = gather[s, pl.ds(0, half)]
 
 
 def allreduce(g1, g2, axis_order, axis_sizes):
@@ -199,10 +252,12 @@
         in_specs=[pl.BlockSpec(memory_space=vmem)] * 2,
         out_specs=[pl.BlockSpec(memory_space=vmem)] * 2,
         scratch_shapes=[
-            vmem((len(steps),) + g1.shape, g1.dtype),
-            vmem((len(steps),) + g2.shape, g2.dtype),
-            pltpu.SemaphoreType.DMA((len(steps), 2)),
-            pltpu.SemaphoreType.DMA((len(steps), 2)),
+            vmem((len(steps), g1.shape[0] // 2) + g1.shape[1:], g1.dtype),
+            vmem((len(steps), g2.shape[0] // 2) + g2.shape[1:], g2.dtype),
+            vmem((len(steps), g1.shape[0] // 2) + g1.shape[1:], g1.dtype),
+            vmem((len(steps), g2.shape[0] // 2) + g2.shape[1:], g2.dtype),
+            pltpu.SemaphoreType.DMA((2 * len(steps), 2)),
+            pltpu.SemaphoreType.DMA((2 * len(steps), 2)),
         ],
         compiler_params=pltpu.CompilerParams(collective_id=0, has_side_effects=True),
     )(g1, g2)

time: 174 us -> 137 us (0.79)
  the two profiles are of different devices: /device:TPU:166 before, /device:TPU:1 now
where the time goes in v4:
time: 137 us
  Pallas kernels  68.3 us (50%)
  waiting for transfers between devices  44.4 us (32%)
  starting transfers between devices  12 us (9%)
  local copies, waits for them, and re-layouts  11.5 us (8%)
    all_to_all x1, waiting for transfers between devices, body(): lax.all_to_all(crops, 'space', split_axis=0, concat_axis=2, tiled=True)  44.4 us
    pallas_call x1, Pallas kernels, allreduce(): pl.pallas_call(functools.partial(allreduce_kernel, axis_order, steps), ou...  43.6 us
    pallas_call x1, Pallas kernels, per_sample(): pl.pallas_call(conv_kernel, out_shape=(jax.ShapeDtypeStruct((c2, planes2...  24.7 us
    all_to_all x1, starting transfers between devices, body(): lax.all_to_all(crops, 'space', split_axis=0, concat_axis=2, tiled=True)  12 us
    pallas_call x2, local copies, waits for them, and re-layouts, allreduce(): pl.pallas_call(functools.partial(allreduce_kernel, axis_order, steps), ou...  3.56 us
  transfers between devices with their start and end apart: 1, of which 1 were waited for; matrix products, arithmetic and copies ran while one was open for 3% of the time, Pallas kernels for 0%

profile of v4, /device:TPU:1, one launch (start us, length us, event | category | flops | bytes accessed | tf_op | source)
XLA Modules:
  0.0 136.9 jit_solution(9286832090960297706)
XLA Ops:
  0.6 0.0 copy-start.2
  0.6 0.0 copy-start.1
  0.7 0.0 copy-start
  0.7 12.0 %all-to-all-start = ((bf16[32,16,2,1024]{3,2,1,0:T(2,128)(2,1)}), bf16[32,16,2,1024]{3,2,1,0:T(2,128)(2,1)S(1)}, u32[]{:S(2)}, u32[]{:S(2)}) async-start(bf16[32,16,2,1024]{3,2,1,0:T(2,128)(2,1)} %param.7), calls=%async_computation | async-start | bytes 4194304 | tf_op jit(solution)/shard_map/all_to_all | solution.py:268
  12.7 0.0 copy-done.2
  12.7 0.7 copy.20.w1_ref
  13.4 0.0 copy-done.1
  13.4 0.8 copy.21.w2_ref
  14.2 0.0 copy-done
  14.2 0.9 reshape_squeeze.3.ogn_ref
  15.0 0.8 copy.18
  15.8 0.2 copy.19
  15.9 0.9 reshape.31.w2t_ref
  16.8 44.4 %all-to-all-done = bf16[32,16,2,1024]{3,2,1,0:T(2,128)(2,1)S(1)} async-done(((bf16[32,16,2,1024]{3,2,1,0:T(2,128)(2,1)}), bf16[32,16,2,1024]{3,2,1,0:T(2,128)(2,1)S(1)}, u32[]{:S(2)}, u32[]{:S(2)}) %all-to-all-start) | async-done | bytes 2097184 | tf_op jit(solution)/shard_map/all_to_all | solution.py:268
  61.2 2.0 %copy.17 = bf16[1,16,32,2,1024]{4,1,3,2,0:T(8,128)(2,1)} copy(bf16[1,16,32,2,1024]{4,3,1,2,0:T(2,128)(2,1)S(1)} %bitcast.26) | data formatting | bytes 4194304 | tf_op jit(solution)/shard_map/all_to_all | solution.py:268
  63.2 24.7 %shard_map.94 = (bf16[64,1024]{1,0:T(8,128)(2,1)}, f32[32,432]{1,0:T(8,128)}, f32[64,864]{1,0:T(8,128)}) custom-call(bf16[64,16,1024]{2,1,0:T(8,128)(2,1)} %bitcast.25, bf16[64,1024]{1,0:T(8,128)(2,1)} %reshape_squeeze.3.ogn_ref, bf16[1024,64]{1,0:T(8,128)(2,1)} %bitcast.27, bf16[32,432]{1,0:T(8,128)(2,1)} %copy.20.w1_ref, bf16[64,864]{1,0:T(8,128)(2,1)} %copy.21.w2_ref, ...), custom_call_target="tpu_custom_call" | custom-call | tf_op jit(solution)/shard_map/pallas_call | solution.py:131
  87.9 1.8 %reshape.32 = bf16[1,64,16,64]{3,2,1,0:T(8,128)(2,1)} reshape(bf16[64,1024]{1,0:T(8,128)(2,1)} %get-tuple-element.8) | data formatting | bytes 262144 | tf_op jit(solution)/shard_map/reshape | solution.py:282
  89.7 43.6 %shard_map.95 = (f32[32,432]{1,0:T(8,128)}, f32[64,864]{1,0:T(8,128)}) custom-call(f32[32,432]{1,0:T(8,128)} %get-tuple-element.9.g1_ref, f32[64,864]{1,0:T(8,128)} %get-tuple-element.10.g2_ref), custom_call_target="tpu_custom_call" | custom-call | tf_op jit(solution)/shard_map/pallas_call | solution.py:249
  133.4 1.7 %copy.22 = f32[32,432]{0,1:T(8,128)} copy(f32[32,432]{1,0:T(8,128)} %get-tuple-element.11) | data formatting | bytes 110592 | tf_op jit(solution)/shard_map/pallas_call | solution.py:249
  135.0 1.9 %copy.23 = f32[64,864]{0,1:T(8,128)} copy(f32[64,864]{1,0:T(8,128)} %get-tuple-element.12) | data formatting | bytes 442368 | tf_op jit(solution)/shard_map/pallas_call | solution.py:249
Async XLA Ops:
  0.6 12.1 %copy-start.2 = (bf16[32,16,3,3,3]{0,1,4,3,2:T(8,128)(2,1)S(1)}, bf16[32,16,3,3,3]{0,1,4,3,2:T(8,128)(2,1)}, u32[]{:S(2)}) copy-start(bf16[32,16,3,3,3]{0,1,4,3,2:T(8,128)(2,1)} %param.8) | copy-start | bytes 82948
  0.6 12.7 %copy-start.1 = (bf16[64,32,3,3,3]{0,1,4,3,2:T(8,128)(2,1)S(1)}, bf16[64,32,3,3,3]{0,1,4,3,2:T(8,128)(2,1)}, u32[]{:S(2)}) copy-start(bf16[64,32,3,3,3]{0,1,4,3,2:T(8,128)(2,1)} %param.9) | copy-start | bytes 331780
  0.7 13.5 %copy-start = (bf16[1,64,16,64]{3,2,1,0:T(8,128)(2,1)S(1)}, bf16[1,64,16,64]{3,2,1,0:T(8,128)(2,1)}, u32[]{:S(2)}) copy-start(bf16[1,64,16,64]{3,2,1,0:T(8,128)(2,1)} %param.10) | copy-start | bytes 393220
  0.7 60.5 %all-to-all-start = ((bf16[32,16,2,1024]{3,2,1,0:T(2,128)(2,1)}), bf16[32,16,2,1024]{3,2,1,0:T(2,128)(2,1)S(1)}, u32[]{:S(2)}, u32[]{:S(2)}) async-start(bf16[32,16,2,1024]{3,2,1,0:T(2,128)(2,1)} %param.7), calls=%async_computation | async-start | bytes 4194304 | tf_op jit(solution)/shard_map/all_to_all | solution.py:268

commit v5 on v4

--- a/solution.py
+++ b/solution.py
@@ -263,10 +263,57 @@
     )(g1, g2)
 
 
+def gather_kernel(axis_order, src_ref, out_ref, send_sem, recv_sem, local_sem):
+    me = {axis: lax.axis_index(axis) for axis in axis_order}
+    n = src_ref.shape[0]
+    planes = src_ref.shape[2]
+    j = me["space"]
+    targets = []
+    for t in range(1, n):
+        there = dict(me)
+        there["space"] = (j + t) % n
+        targets.append((t, there["space"], tuple(there[a] for a in axis_order)))
+
+    barrier = pltpu.get_barrier_semaphore()
+    for t, dest, device in targets:
+        pl.semaphore_signal(barrier, 1, device_id=device, device_id_type=pl.DeviceIdType.MESH)
+    pl.semaphore_wait(barrier, n - 1)
+
+    mine = pl.ds(pl.multiple_of(j * planes, planes), planes)
+    local = pltpu.make_async_copy(src_ref.at[j], out_ref.at[:, mine, :], local_sem)
+    local.start()
+    copies = []
+    for t, dest, device in targets:
+        copy = pltpu.make_async_remote_copy(
+            src_ref=src_ref.at[dest], dst_ref=out_ref.at[:, mine, :],
+            send_sem=send_sem.at[t], recv_sem=recv_sem.at[t],
+            device_id=device, device_id_type=pl.DeviceIdType.MESH)
+        copy.start()
+        copies.append(copy)
+    local.wait()
+    for copy in copies:
+        copy.wait()
+
+
+def gather_crops(crops, axis_order):
+    n, c0, planes, cells = crops.shape
+    return pl.pallas_call(
+        functools.partial(gather_kernel, axis_order),
+        out_shape=jax.ShapeDtypeStruct((c0, n * planes, cells), crops.dtype),
+        in_specs=[pl.BlockSpec(memory_space=pl.ANY)],
+        out_specs=pl.BlockSpec(memory_space=pl.ANY),
+        scratch_shapes=[
+            pltpu.SemaphoreType.DMA((n,)),
+            pltpu.SemaphoreType.DMA((n,)),
+            pltpu.SemaphoreType.DMA(()),
+        ],
+        compiler_params=pltpu.CompilerParams(collective_id=1, has_side_effects=True),
+    )(crops)
+
+
 def body(axis_order, axis_sizes, crops, first_kernel, second_kernel, out_grad):
     local_samples, channels_in, planes, flat_cells = crops.shape
-    whole_input = lax.all_to_all(crops, "space", split_axis=0, concat_axis=2, tiled=True)
-    x = whole_input[0].transpose(1, 0, 2)
+    x = gather_crops(crops, axis_order).transpose(1, 0, 2)
     c1, c2 = first_kernel.shape[0], second_kernel.shape[0]
     og = out_grad[0]
     ogn = og.reshape(c2, -1)

time: 137 us -> 143 us (1.044)
  Pallas kernels: 68.3 us -> 128 us
  waiting for transfers between devices: 44.4 us -> 0 us
  starting transfers between devices: 12 us -> 0 us
  local copies, waits for them, and re-layouts: 11.5 us -> 13.6 us
    pallas_call x0 -> x1, Pallas kernels: none -> 56.4 us  [gather_crops(): pl.pallas_call(functools.partial(gather_kernel, axis_order), out_shape=ja...]
    all_to_all x1 -> x0, waiting for transfers between devices: 44.4 us -> none  [body(): lax.all_to_all(crops, 'space', split_axis=0, concat_axis=2, tiled=True)]
    all_to_all x1 -> x0, starting transfers between devices: 12 us -> none  [body(): lax.all_to_all(crops, 'space', split_axis=0, concat_axis=2, tiled=True)]
    pallas_call x0 -> x1, local copies, waits for them, and re-layouts: none -> 4.12 us  [gather_crops(): pl.pallas_call(functools.partial(gather_kernel, axis_order), out_shape=ja...]
    pallas_call x1, Pallas kernels: 43.6 us -> 47.2 us  [allreduce(): pl.pallas_call(functools.partial(allreduce_kernel, axis_order, steps), ou...]
    all_to_all x1 -> x0, local copies, waits for them, and re-layouts: 2.03 us -> none  [body(): lax.all_to_all(crops, 'space', split_axis=0, concat_axis=2, tiled=True)]
  transfers between devices with their start and end apart: 1 -> 0, of which waited for: 1 -> 0; matrix products, arithmetic and copies ran while one was open for 3% -> 0% of each run, Pallas kernels for 0% -> 0%
where the time goes in v5:
time: 143 us
  Pallas kernels  128 us (90%)
  local copies, waits for them, and re-layouts  13.6 us (10%)
    pallas_call x1, Pallas kernels, gather_crops(): pl.pallas_call(functools.partial(gather_kernel, axis_order), out_shape=ja...  56.4 us
    pallas_call x1, Pallas kernels, allreduce(): pl.pallas_call(functools.partial(allreduce_kernel, axis_order, steps), ou...  47.2 us
    pallas_call x1, Pallas kernels, per_sample(): pl.pallas_call(conv_kernel, out_shape=(jax.ShapeDtypeStruct((c2, planes2...  24.7 us
    pallas_call x1, local copies, waits for them, and re-layouts, gather_crops(): pl.pallas_call(functools.partial(gather_kernel, axis_order), out_shape=ja...  4.12 us
    pallas_call x2, local copies, waits for them, and re-layouts, allreduce(): pl.pallas_call(functools.partial(allreduce_kernel, axis_order, steps), ou...  3.56 us

profile of v5, /device:TPU:1, one launch (start us, length us, event | category | flops | bytes accessed | tf_op | source)
XLA Modules:
  0.0 142.5 jit_solution(16697127413509972535)
XLA Ops:
  0.6 56.4 %shard_map.94 = bf16[16,64,1024]{2,1,0:T(8,128)(2,1)} custom-call(bf16[32,16,2,1024]{3,2,1,0:T(2,128)(2,1)} %src_ref.1), custom_call_target="tpu_custom_call" | custom-call | tf_op jit(solution)/shard_map/pallas_call | solution.py:300
  57.0 0.0 copy-start.1
  57.0 0.0 copy-start
  57.0 4.1 %copy.25 = bf16[16,64,1024]{2,0,1:T(8,128)(2,1)} copy(bf16[16,64,1024]{2,1,0:T(8,128)(2,1)} %shard_map.94) | data formatting | bytes 4194304 | tf_op jit(solution)/shard_map/pallas_call | solution.py:300
  61.1 0.0 copy-start.2
  61.1 0.0 copy-done.1
  61.1 0.2 copy.19
  61.3 0.9 reshape.30.w2t_ref
  62.2 0.0 copy-done
  62.2 0.8 copy.18
  62.9 0.9 reshape_squeeze.3.ogn_ref
  63.8 0.8 copy.21.w2_ref
  64.6 0.0 copy-done.2
  64.6 0.7 copy.20.w1_ref
  65.3 24.7 %shard_map.95 = (bf16[64,1024]{1,0:T(8,128)(2,1)}, f32[32,432]{1,0:T(8,128)}, f32[64,864]{1,0:T(8,128)}) custom-call(bf16[64,16,1024]{2,1,0:T(8,128)(2,1)} %bitcast.22, bf16[64,1024]{1,0:T(8,128)(2,1)} %reshape_squeeze.3.ogn_ref, bf16[1024,64]{1,0:T(8,128)(2,1)} %bitcast.23, bf16[32,432]{1,0:T(8,128)(2,1)} %copy.20.w1_ref, bf16[64,864]{1,0:T(8,128)(2,1)} %copy.21.w2_ref, ...), custom_call_target="tpu_custom_call" | custom-call | tf_op jit(solution)/shard_map/pallas_call | solution.py:131
  90.0 47.2 %shard_map.96 = (f32[32,432]{1,0:T(8,128)}, f32[64,864]{1,0:T(8,128)}) custom-call(f32[32,432]{1,0:T(8,128)} %get-tuple-element.9.g1_ref, f32[64,864]{1,0:T(8,128)} %get-tuple-element.10.g2_ref), custom_call_target="tpu_custom_call" | custom-call | tf_op jit(solution)/shard_map/pallas_call | solution.py:249
  137.2 1.9 %copy.23 = f32[64,864]{0,1:T(8,128)} copy(f32[64,864]{1,0:T(8,128)} %get-tuple-element.12) | data formatting | bytes 442368 | tf_op jit(solution)/shard_map/pallas_call | solution.py:249
  139.1 1.7 %copy.22 = f32[32,432]{0,1:T(8,128)} copy(f32[32,432]{1,0:T(8,128)} %get-tuple-element.11) | data formatting | bytes 110592 | tf_op jit(solution)/shard_map/pallas_call | solution.py:249
  140.7 1.8 %reshape.31 = bf16[1,64,16,64]{3,2,1,0:T(8,128)(2,1)} reshape(bf16[64,1024]{1,0:T(8,128)(2,1)} %get-tuple-element.8) | data formatting | bytes 262144 | tf_op jit(solution)/shard_map/reshape | solution.py:329
Async XLA Ops:
  57.0 4.2 %copy-start.1 = (bf16[64,32,3,3,3]{0,1,4,3,2:T(8,128)(2,1)S(1)}, bf16[64,32,3,3,3]{0,1,4,3,2:T(8,128)(2,1)}, u32[]{:S(2)}) copy-start(bf16[64,32,3,3,3]{0,1,4,3,2:T(8,128)(2,1)} %param.9) | copy-start | bytes 331780
  57.0 5.2 %copy-start = (bf16[1,64,16,64]{3,2,1,0:T(8,128)(2,1)S(1)}, bf16[1,64,16,64]{3,2,1,0:T(8,128)(2,1)}, u32[]{:S(2)}) copy-start(bf16[1,64,16,64]{3,2,1,0:T(8,128)(2,1)} %param.10) | copy-start | bytes 393220
  61.1 3.4 %copy-start.2 = (bf16[32,16,3,3,3]{0,1,4,3,2:T(8,128)(2,1)S(1)}, bf16[32,16,3,3,3]{0,1,4,3,2:T(8,128)(2,1)}, u32[]{:S(2)}) copy-start(bf16[32,16,3,3,3]{0,1,4,3,2:T(8,128)(2,1)} %param.8) | copy-start | bytes 82948

commit v6 on v4

--- a/solution.py
+++ b/solution.py
@@ -70,8 +70,8 @@
                             val = val + q1_ref[2 * pd + a, :, pl.ds((h_lo * 3 + c) * 128, 128)].astype(jnp.float32)
                         s_ref[pd, pl.ds(r0, c0), pl.ds(m * 128, 128)] = val.astype(s_ref.dtype)
         pre = jnp.dot(w1_ref[...], s_ref[pd], preferred_element_type=jnp.float32)
-        fp_ref[pd] = pre
         sig = 1.0 / (1.0 + jnp.exp(-pre))
+        fp_ref[pd] = sig * (1.0 + pre * (1.0 - sig))
         a2_ref[pd + 1] = (pre * sig).astype(a2_ref.dtype)
         return carry
 
@@ -111,9 +111,7 @@
                + jnp.dot(w2t_ref[0], vq1, preferred_element_type=jnp.float32))
         for k, act in ((0, even), (1, odd)):
             d2 = 2 * q + k
-            pre = fp_ref[d2]
-            sig = 1.0 / (1.0 + jnp.exp(-pre))
-            slope = sig * (1.0 + pre * (1.0 - sig))
+            slope = fp_ref[d2]
             pg = (act.astype(jnp.bfloat16).astype(jnp.float32) * slope).astype(jnp.bfloat16)
             fg_ref[...] += lax.dot_general(pg, s_ref[d2], NT, preferred_element_type=jnp.float32)
         return carry
@@ -173,8 +171,8 @@
     return count
 
 
-def allreduce_kernel(axis_order, steps, g1_ref, g2_ref, o1_ref, o2_ref, r1_ref, r2_ref, a1_ref, a2_ref,
-                     send_sem, recv_sem):
+def allreduce_kernel(axis_order, steps, g1_ref, g2_ref, t1_ref, t2_ref, o1_ref, o2_ref, r1_ref, r2_ref,
+                     a1_ref, a2_ref, send_sem, recv_sem):
     me = {axis: lax.axis_index(axis) for axis in axis_order}
     partners, bits = [], []
     for axis, bit in steps:
@@ -241,6 +239,8 @@
             copy.wait()
         for acc, gather, give, half in places:
             acc[pl.ds(give, half)] = gather[s, pl.ds(0, half)]
+    t1_ref[...] = o1_ref[...].T
+    t2_ref[...] = o2_ref[...].T
 
 
 def allreduce(g1, g2, axis_order, axis_sizes):
@@ -248,10 +248,12 @@
     vmem = pltpu.VMEM
     return pl.pallas_call(
         functools.partial(allreduce_kernel, axis_order, steps),
-        out_shape=(jax.ShapeDtypeStruct(g1.shape, g1.dtype), jax.ShapeDtypeStruct(g2.shape, g2.dtype)),
+        out_shape=(jax.ShapeDtypeStruct(g1.shape[::-1], g1.dtype), jax.ShapeDtypeStruct(g2.shape[::-1], g2.dtype)),
         in_specs=[pl.BlockSpec(memory_space=vmem)] * 2,
         out_specs=[pl.BlockSpec(memory_space=vmem)] * 2,
         scratch_shapes=[
+            vmem(g1.shape, g1.dtype),
+            vmem(g2.shape, g2.dtype),
             vmem((len(steps), g1.shape[0] // 2) + g1.shape[1:], g1.dtype),
             vmem((len(steps), g2.shape[0] // 2) + g2.shape[1:], g2.dtype),
             vmem((len(steps), g1.shape[0] // 2) + g1.shape[1:], g1.dtype),
@@ -281,8 +283,8 @@
     )
     features_out = feat.reshape(out_grad.shape)
     fg, sg = allreduce(fg, sg, axis_order, axis_sizes)
-    first_grad = fg.reshape(c1, 3, 3, 3, channels_in).transpose(0, 4, 1, 2, 3)
-    second_grad = sg.reshape(c2, 3, 3, 3, c1).transpose(0, 4, 1, 2, 3)
+    first_grad = fg.reshape(3, 3, 3, channels_in, c1).transpose(4, 3, 0, 1, 2)
+    second_grad = sg.reshape(3, 3, 3, c1, c2).transpose(4, 3, 0, 1, 2)
     return (features_out, first_grad, second_grad)
 
 

time: 137 us -> 137 us (level)
    pallas_call x2 -> x0, local copies, waits for them, and re-layouts: 3.56 us -> none  [allreduce(): pl.pallas_call(functools.partial(allreduce_kernel, axis_order, steps), ou...]
    unnamed x6 -> x8, local copies, waits for them, and re-layouts: 0.01 us -> 3.45 us
where the time goes in v6:
time: 137 us
  Pallas kernels  68.7 us (50%)
  waiting for transfers between devices  44.4 us (32%)
  starting transfers between devices  12 us (9%)
  local copies, waits for them, and re-layouts  11.4 us (8%)
    all_to_all x1, waiting for transfers between devices, body(): lax.all_to_all(crops, 'space', split_axis=0, concat_axis=2, tiled=True)  44.4 us
    pallas_call x1, Pallas kernels, allreduce(): pl.pallas_call(functools.partial(allreduce_kernel, axis_order, steps), ou...  43.9 us
    pallas_call x1, Pallas kernels, per_sample(): pl.pallas_call(conv_kernel, out_shape=(jax.ShapeDtypeStruct((c2, planes2...  24.8 us
    all_to_all x1, starting transfers between devices, body(): lax.all_to_all(crops, 'space', split_axis=0, concat_axis=2, tiled=True)  12 us
    unnamed x8, local copies, waits for them, and re-layouts  3.45 us
  transfers between devices with their start and end apart: 1, of which 1 were waited for; matrix products, arithmetic and copies ran while one was open for 3% of the time, Pallas kernels for 0%

profile of v6, /device:TPU:1, one launch (start us, length us, event | category | flops | bytes accessed | tf_op | source)
XLA Modules:
  0.0 137.2 jit_solution(14503701076792530415)
XLA Ops:
  0.6 0.0 copy-start.2
  0.6 0.0 copy-start.1
  0.7 0.0 copy-start
  0.7 12.0 %all-to-all-start = ((bf16[32,16,2,1024]{3,2,1,0:T(2,128)(2,1)}), bf16[32,16,2,1024]{3,2,1,0:T(2,128)(2,1)S(1)}, u32[]{:S(2)}, u32[]{:S(2)}) async-start(bf16[32,16,2,1024]{3,2,1,0:T(2,128)(2,1)} %param.7), calls=%async_computation | async-start | bytes 4194304 | tf_op jit(solution)/shard_map/all_to_all | solution.py:270
  12.7 0.0 copy-done.2
  12.7 0.7 copy.18.w1_ref
  13.4 0.0 copy-done.1
  13.4 0.8 copy.19.w2_ref
  14.2 0.0 copy-done
  14.2 0.9 reshape_squeeze.3.ogn_ref
  15.0 0.8 copy.16
  15.8 0.2 copy.17
  15.9 0.9 reshape.31.w2t_ref
  16.8 44.4 %all-to-all-done = bf16[32,16,2,1024]{3,2,1,0:T(2,128)(2,1)S(1)} async-done(((bf16[32,16,2,1024]{3,2,1,0:T(2,128)(2,1)}), bf16[32,16,2,1024]{3,2,1,0:T(2,128)(2,1)S(1)}, u32[]{:S(2)}, u32[]{:S(2)}) %all-to-all-start) | async-done | bytes 2097184 | tf_op jit(solution)/shard_map/all_to_all | solution.py:270
  61.2 2.0 %copy.15 = bf16[1,16,32,2,1024]{4,1,3,2,0:T(8,128)(2,1)} copy(bf16[1,16,32,2,1024]{4,3,1,2,0:T(2,128)(2,1)S(1)} %bitcast.26) | data formatting | bytes 4194304 | tf_op jit(solution)/shard_map/all_to_all | solution.py:270
  63.2 24.8 %shard_map.94 = (bf16[64,1024]{1,0:T(8,128)(2,1)}, f32[32,432]{1,0:T(8,128)}, f32[64,864]{1,0:T(8,128)}) custom-call(bf16[64,16,1024]{2,1,0:T(8,128)(2,1)} %bitcast.25, bf16[64,1024]{1,0:T(8,128)(2,1)} %reshape_squeeze.3.ogn_ref, bf16[1024,64]{1,0:T(8,128)(2,1)} %bitcast.27, bf16[32,432]{1,0:T(8,128)(2,1)} %copy.18.w1_ref, bf16[64,864]{1,0:T(8,128)(2,1)} %copy.19.w2_ref, ...), custom_call_target="tpu_custom_call" | custom-call | tf_op jit(solution)/shard_map/pallas_call | solution.py:129
  88.0 1.8 %reshape.32 = bf16[1,64,16,64]{3,2,1,0:T(8,128)(2,1)} reshape(bf16[64,1024]{1,0:T(8,128)(2,1)} %get-tuple-element.8) | data formatting | bytes 262144 | tf_op jit(solution)/shard_map/reshape | solution.py:284
  89.8 43.9 %shard_map.95 = (f32[432,32]{1,0:T(8,128)}, f32[864,64]{1,0:T(8,128)}) custom-call(f32[32,432]{1,0:T(8,128)} %get-tuple-element.9.g1_ref, f32[64,864]{1,0:T(8,128)} %get-tuple-element.10.g2_ref), custom_call_target="tpu_custom_call" | custom-call | tf_op jit(solution)/shard_map/pallas_call | solution.py:249
  133.7 1.6 %copy.22 = f32[32,16,3,3,3]{0,1,4,3,2:T(8,128)} copy(f32[32,16,3,3,3]{0,1,4,3,2:T(8,128)} %bitcast.32) | data formatting | bytes 110592
  135.4 1.8 %copy.23 = f32[64,32,3,3,3]{0,1,4,3,2:T(8,128)} copy(f32[64,32,3,3,3]{0,1,4,3,2:T(8,128)} %bitcast.31) | data formatting | bytes 442368
Async XLA Ops:
  0.6 12.1 %copy-start.2 = (bf16[32,16,3,3,3]{0,1,4,3,2:T(8,128)(2,1)S(1)}, bf16[32,16,3,3,3]{0,1,4,3,2:T(8,128)(2,1)}, u32[]{:S(2)}) copy-start(bf16[32,16,3,3,3]{0,1,4,3,2:T(8,128)(2,1)} %param.8) | copy-start | bytes 82948
  0.6 12.7 %copy-start.1 = (bf16[64,32,3,3,3]{0,1,4,3,2:T(8,128)(2,1)S(1)}, bf16[64,32,3,3,3]{0,1,4,3,2:T(8,128)(2,1)}, u32[]{:S(2)}) copy-start(bf16[64,32,3,3,3]{0,1,4,3,2:T(8,128)(2,1)} %param.9) | copy-start | bytes 331780
  0.7 13.5 %copy-start = (bf16[1,64,16,64]{3,2,1,0:T(8,128)(2,1)S(1)}, bf16[1,64,16,64]{3,2,1,0:T(8,128)(2,1)}, u32[]{:S(2)}) copy-start(bf16[1,64,16,64]{3,2,1,0:T(8,128)(2,1)} %param.10) | copy-start | bytes 393220
  0.7 60.5 %all-to-all-start = ((bf16[32,16,2,1024]{3,2,1,0:T(2,128)(2,1)}), bf16[32,16,2,1024]{3,2,1,0:T(2,128)(2,1)S(1)}, u32[]{:S(2)}, u32[]{:S(2)}) async-start(bf16[32,16,2,1024]{3,2,1,0:T(2,128)(2,1)} %param.7), calls=%async_computation | async-start | bytes 4194304 | tf_op jit(solution)/shard_map/all_to_all | solution.py:270

commit v7 on v6

--- a/solution.py
+++ b/solution.py
@@ -148,118 +148,164 @@
     )(x, ogn, ogq, w1, w2, w2t, t1, sel2, up)
 
 
-STEP_ORDER = (("sample", 1), ("space", 4), ("sample", 2), ("space", 1),
-              ("space", 2), ("sample", 4), ("space", 8), ("space", 16))
-
-
-def partner_steps(axis_sizes):
+ROUND_ORDER = ((("sample", 1),), (("space", 4),), (("sample", 2),),
+               (("space", 1), ("space", 2), ("sample", 4)), (("space", 8), ("space", 16)))
+
+
+def exchange_rounds(axis_sizes):
     sizes = dict(axis_sizes)
-    steps = [(axis, bit) for axis, bit in STEP_ORDER if bit < sizes[axis]]
+    rounds = []
+    for group in ROUND_ORDER:
+        kept = tuple((axis, bit) for axis, bit in group if bit < sizes[axis])
+        if kept:
+            rounds.append(kept)
+    used = {pair for group in rounds for pair in group}
     for axis, size in axis_sizes:
         bit = 1
         while bit < size:
-            if (axis, bit) not in steps:
-                steps.append((axis, bit))
+            if (axis, bit) not in used:
+                rounds.append(((axis, bit),))
             bit *= 2
-    return steps
-
-
-def halvings(rows, steps):
+    return rounds
+
+
+def halvings(rows, rounds):
     count = 0
-    while count < len(steps) and rows % (2 ** (count + 1) * 8) == 0:
+    while (count < len(rounds) and len(rounds[count]) == 1
+           and rows % (2 ** (count + 1) * 8) == 0):
         count += 1
     return count
 
 
-def allreduce_kernel(axis_order, steps, g1_ref, g2_ref, t1_ref, t2_ref, o1_ref, o2_ref, r1_ref, r2_ref,
-                     a1_ref, a2_ref, send_sem, recv_sem):
+def allreduce_kernel(axis_order, rounds, g1_ref, g2_ref, t1_ref, t2_ref, o1_ref, o2_ref, r1_ref, r2_ref,
+                     a1_ref, a2_ref, x1_ref, x2_ref, send_sem, recv_sem, gather_sem):
     me = {axis: lax.axis_index(axis) for axis in axis_order}
-    partners, bits = [], []
-    for axis, bit in steps:
-        mine = (me[axis] // bit) % 2
-        there = dict(me)
-        there[axis] = me[axis] + bit - 2 * bit * mine
-        partners.append(tuple(there[a] for a in axis_order))
-        bits.append(mine)
+
+    def bit_of(axis, bit):
+        return (me[axis] // bit) % 2
+
+    plan_rounds = []
+    for group in rounds:
+        own = sum(bit_of(axis, bit) * 2 ** idx for idx, (axis, bit) in enumerate(group))
+        members = []
+        for t in range(1, 2 ** len(group)):
+            there = dict(me)
+            slot = 0
+            for idx, (axis, bit) in enumerate(group):
+                flip = (t // 2 ** idx) % 2
+                if flip:
+                    there[axis] = there[axis] + bit - 2 * bit * bit_of(axis, bit)
+                slot = slot + ((bit_of(axis, bit) + flip) % 2) * 2 ** idx
+            members.append((t, slot, tuple(there[a] for a in axis_order)))
+        plan_rounds.append((group, own, members))
 
     barrier = pltpu.get_barrier_semaphore()
-    for partner in partners:
-        pl.semaphore_signal(barrier, 1, device_id=partner, device_id_type=pl.DeviceIdType.MESH)
-    pl.semaphore_wait(barrier, len(partners))
+    count = 0
+    for group, own, members in plan_rounds:
+        for t, slot, device in members:
+            pl.semaphore_signal(barrier, 1, device_id=device, device_id_type=pl.DeviceIdType.MESH)
+            count += 1
+    pl.semaphore_wait(barrier, count)
 
     accs = (o1_ref, o2_ref)
     recvs = (r1_ref, r2_ref)
     gathers = (a1_ref, a2_ref)
+    groups = (x1_ref, x2_ref)
     o1_ref[...] = g1_ref[...]
     o2_ref[...] = g2_ref[...]
-    n_steps = len(steps)
-    plans = []
-    for acc in accs:
-        plans.append({"rows": acc.shape[0], "h": halvings(acc.shape[0], steps), "off": 0, "kept": []})
-
-    def remote(src, dst, slot, k, partner):
+    plans = [{"rows": acc.shape[0], "h": halvings(acc.shape[0], rounds), "off": 0, "kept": []} for acc in accs]
+
+    def remote(src, dst, send, recv, device):
         return pltpu.make_async_remote_copy(
-            src_ref=src, dst_ref=dst, send_sem=send_sem.at[slot, k], recv_sem=recv_sem.at[slot, k],
-            device_id=partner, device_id_type=pl.DeviceIdType.MESH)
-
-    for s in range(n_steps):
-        copies, adds = [], []
-        for k, (acc, recv, plan) in enumerate(zip(accs, recvs, plans)):
-            if s < plan["h"]:
+            src_ref=src, dst_ref=dst, send_sem=send, recv_sem=recv,
+            device_id=device, device_id_type=pl.DeviceIdType.MESH)
+
+    for r, (group, own, members) in enumerate(plan_rounds):
+        sends, recvs_wait, after = [], [], []
+        for k, (acc, recv, xbuf, plan) in enumerate(zip(accs, recvs, groups, plans)):
+            if r < plan["h"]:
+                (axis, bit), = group
+                t, slot, device = members[0]
+                mine = bit_of(axis, bit)
                 half = plan["rows"] // 2
-                keep = pl.multiple_of(plan["off"] + bits[s] * half, 8)
-                give = pl.multiple_of(plan["off"] + (1 - bits[s]) * half, 8)
-                copies.append(remote(acc.at[pl.ds(give, half)], recv.at[s, pl.ds(0, half)], s, k, partners[s]))
-                adds.append((acc, recv, s, keep, half))
-                plan["kept"].append((s, keep, give, half))
+                keep = pl.multiple_of(plan["off"] + mine * half, 8)
+                give = pl.multiple_of(plan["off"] + (1 - mine) * half, 8)
+                copy = remote(acc.at[pl.ds(give, half)], recv.at[r, pl.ds(0, half)],
+                              send_sem.at[r, 0, k], recv_sem.at[r, 0, k], device)
+                sends.append(copy)
+                recvs_wait.append(copy)
+                after.append(("add", acc, recv, r, keep, half))
+                plan["kept"].append((r, keep, give, half))
                 plan["off"], plan["rows"] = keep, half
             else:
-                rows = plan["rows"]
-                off = plan["off"]
-                copies.append(remote(acc.at[pl.ds(off, rows)], recv.at[s, pl.ds(0, rows)], s, k, partners[s]))
-                adds.append((acc, recv, s, off, rows))
-        for copy in copies:
+                rows, off = plan["rows"], plan["off"]
+                xbuf[r, own] = acc[pl.ds(off, rows)]
+                for t, slot, device in members:
+                    sends.append(remote(acc.at[pl.ds(off, rows)], xbuf.at[r, own],
+                                        send_sem.at[r, t, k], recv_sem.at[r, own, k], device))
+                    recvs_wait.append(remote(acc.at[pl.ds(off, rows)], xbuf.at[r, slot],
+                                             send_sem.at[r, t, k], recv_sem.at[r, slot, k], device))
+                after.append(("sum", acc, xbuf, r, off, rows, 2 ** len(group)))
+        for copy in sends:
             copy.start()
-        for copy in copies:
-            copy.wait()
-        for acc, recv, slot, off, rows in adds:
-            acc[pl.ds(off, rows)] = acc[pl.ds(off, rows)] + recv[slot, pl.ds(0, rows)]
-
-    for s in reversed(range(n_steps)):
+        for copy in sends:
+            copy.wait_send()
+        for copy in recvs_wait:
+            copy.wait_recv()
+        for item in after:
+            if item[0] == "add":
+                _, acc, recv, slot_r, off, rows = item
+                acc[pl.ds(off, rows)] = acc[pl.ds(off, rows)] + recv[slot_r, pl.ds(0, rows)]
+            else:
+                _, acc, xbuf, slot_r, off, rows, n_members = item
+                total = xbuf[slot_r, 0]
+                for q in range(1, n_members):
+                    total = total + xbuf[slot_r, q]
+                acc[pl.ds(off, rows)] = total
+
+    for r in reversed(range(len(plan_rounds))):
         copies, places = [], []
+        group, own, members = plan_rounds[r]
         for k, (acc, gather, plan) in enumerate(zip(accs, gathers, plans)):
             for step, keep, give, half in plan["kept"]:
-                if step == s:
-                    copies.append(remote(acc.at[pl.ds(keep, half)], gather.at[s, pl.ds(0, half)],
-                                         n_steps + s, k, partners[s]))
+                if step == r:
+                    t, slot, device = members[0]
+                    copies.append(remote(acc.at[pl.ds(keep, half)], gather.at[r, pl.ds(0, half)],
+                                         gather_sem.at[r, 0, k], gather_sem.at[r, 1, k], device))
                     places.append((acc, gather, give, half))
         for copy in copies:
             copy.start()
         for copy in copies:
             copy.wait()
         for acc, gather, give, half in places:
-            acc[pl.ds(give, half)] = gather[s, pl.ds(0, half)]
+            acc[pl.ds(give, half)] = gather[r, pl.ds(0, half)]
     t1_ref[...] = o1_ref[...].T
     t2_ref[...] = o2_ref[...].T
 
 
 def allreduce(g1, g2, axis_order, axis_sizes):
-    steps = partner_steps(axis_sizes)
+    rounds = exchange_rounds(axis_sizes)
+    n = len(rounds)
+    width = max(2 ** len(group) for group in rounds)
     vmem = pltpu.VMEM
+    chunk = [g.shape[0] // 2 ** halvings(g.shape[0], rounds) for g in (g1, g2)]
     return pl.pallas_call(
-        functools.partial(allreduce_kernel, axis_order, steps),
+        functools.partial(allreduce_kernel, axis_order, rounds),
         out_shape=(jax.ShapeDtypeStruct(g1.shape[::-1], g1.dtype), jax.ShapeDtypeStruct(g2.shape[::-1], g2.dtype)),
         in_specs=[pl.BlockSpec(memory_space=vmem)] * 2,
         out_specs=[pl.BlockSpec(memory_space=vmem)] * 2,
         scratch_shapes=[
             vmem(g1.shape, g1.dtype),
             vmem(g2.shape, g2.dtype),
-            vmem((len(steps), g1.shape[0] // 2) + g1.shape[1:], g1.dtype),
-            vmem((len(steps), g2.shape[0] // 2) + g2.shape[1:], g2.dtype),
-            vmem((len(steps), g1.shape[0] // 2) + g1.shape[1:], g1.dtype),
-            vmem((len(steps), g2.shape[0] // 2) + g2.shape[1:], g2.dtype),
-            pltpu.SemaphoreType.DMA((2 * len(steps), 2)),
-            pltpu.SemaphoreType.DMA((2 * len(steps), 2)),
+            vmem((n, g1.shape[0] // 2) + g1.shape[1:], g1.dtype),
+            vmem((n, g2.shape[0] // 2) + g2.shape[1:], g2.dtype),
+            vmem((n, g1.shape[0] // 2) + g1.shape[1:], g1.dtype),
+            vmem((n, g2.shape[0] // 2) + g2.shape[1:], g2.dtype),
+            vmem((n, width, chunk[0]) + g1.shape[1:], g1.dtype),
+            vmem((n, width, chunk[1]) + g2.shape[1:], g2.dtype),
+            pltpu.SemaphoreType.DMA((n, width, 2)),
+            pltpu.SemaphoreType.DMA((n, width, 2)),
+            pltpu.SemaphoreType.DMA((n, 2, 2)),
         ],
         compiler_params=pltpu.CompilerParams(collective_id=0, has_side_effects=True),
     )(g1, g2)

time: 137 us -> 132 us (0.964)
  Pallas kernels: 68.7 us -> 63.6 us
    pallas_call x1, Pallas kernels: 43.9 us -> 38.8 us  [allreduce(): pl.pallas_call(functools.partial(allreduce_kernel, axis_order, rounds), o...]
where the time goes in v7:
time: 132 us
  Pallas kernels  63.6 us (48%)
  waiting for transfers between devices  44.4 us (34%)
  starting transfers between devices  12 us (9%)
  local copies, waits for them, and re-layouts  11.4 us (9%)
    all_to_all x1, waiting for transfers between devices, body(): lax.all_to_all(crops, 'space', split_axis=0, concat_axis=2, tiled=True)  44.4 us
    pallas_call x1, Pallas kernels, allreduce(): pl.pallas_call(functools.partial(allreduce_kernel, axis_order, rounds), o...  38.8 us
    pallas_call x1, Pallas kernels, per_sample(): pl.pallas_call(conv_kernel, out_shape=(jax.ShapeDtypeStruct((c2, planes2...  24.8 us
    all_to_all x1, starting transfers between devices, body(): lax.all_to_all(crops, 'space', split_axis=0, concat_axis=2, tiled=True)  12 us
    unnamed x8, local copies, waits for them, and re-layouts  3.45 us
  transfers between devices with their start and end apart: 1, of which 1 were waited for; matrix products, arithmetic and copies ran while one was open for 3% of the time, Pallas kernels for 0%

profile of v7, /device:TPU:1, one launch (start us, length us, event | category | flops | bytes accessed | tf_op | source)
XLA Modules:
  0.0 132.0 jit_solution(10046485293764249959)
XLA Ops:
  0.6 0.0 copy-start.2
  0.6 0.0 copy-start.1
  0.7 0.0 copy-start
  0.7 12.0 %all-to-all-start = ((bf16[32,16,2,1024]{3,2,1,0:T(2,128)(2,1)}), bf16[32,16,2,1024]{3,2,1,0:T(2,128)(2,1)S(1)}, u32[]{:S(2)}, u32[]{:S(2)}) async-start(bf16[32,16,2,1024]{3,2,1,0:T(2,128)(2,1)} %param.7), calls=%async_computation | async-start | bytes 4194304 | tf_op jit(solution)/shard_map/all_to_all | solution.py:316
  12.7 0.0 copy-done.2
  12.7 0.7 copy.18.w1_ref
  13.4 0.0 copy-done.1
  13.4 0.8 copy.19.w2_ref
  14.2 0.0 copy-done
  14.2 0.9 reshape_squeeze.3.ogn_ref
  15.0 0.8 copy.16
  15.8 0.2 copy.17
  15.9 0.9 reshape.31.w2t_ref
  16.8 44.4 %all-to-all-done = bf16[32,16,2,1024]{3,2,1,0:T(2,128)(2,1)S(1)} async-done(((bf16[32,16,2,1024]{3,2,1,0:T(2,128)(2,1)}), bf16[32,16,2,1024]{3,2,1,0:T(2,128)(2,1)S(1)}, u32[]{:S(2)}, u32[]{:S(2)}) %all-to-all-start) | async-done | bytes 2097184 | tf_op jit(solution)/shard_map/all_to_all | solution.py:316
  61.2 2.0 %copy.15 = bf16[1,16,32,2,1024]{4,1,3,2,0:T(8,128)(2,1)} copy(bf16[1,16,32,2,1024]{4,3,1,2,0:T(2,128)(2,1)S(1)} %bitcast.26) | data formatting | bytes 4194304 | tf_op jit(solution)/shard_map/all_to_all | solution.py:316
  63.2 24.8 %shard_map.94 = (bf16[64,1024]{1,0:T(8,128)(2,1)}, f32[32,432]{1,0:T(8,128)}, f32[64,864]{1,0:T(8,128)}) custom-call(bf16[64,16,1024]{2,1,0:T(8,128)(2,1)} %bitcast.25, bf16[64,1024]{1,0:T(8,128)(2,1)} %reshape_squeeze.3.ogn_ref, bf16[1024,64]{1,0:T(8,128)(2,1)} %bitcast.27, bf16[32,432]{1,0:T(8,128)(2,1)} %copy.18.w1_ref, bf16[64,864]{1,0:T(8,128)(2,1)} %copy.19.w2_ref, ...), custom_call_target="tpu_custom_call" | custom-call | tf_op jit(solution)/shard_map/pallas_call | solution.py:129
  88.0 1.8 %reshape.32 = bf16[1,64,16,64]{3,2,1,0:T(8,128)(2,1)} reshape(bf16[64,1024]{1,0:T(8,128)(2,1)} %get-tuple-element.8) | data formatting | bytes 262144 | tf_op jit(solution)/shard_map/reshape | solution.py:330
  89.8 38.8 %shard_map.95 = (f32[432,32]{1,0:T(8,128)}, f32[864,64]{1,0:T(8,128)}) custom-call(f32[32,432]{1,0:T(8,128)} %get-tuple-element.9.g1_ref, f32[64,864]{1,0:T(8,128)} %get-tuple-element.10.g2_ref), custom_call_target="tpu_custom_call" | custom-call | tf_op jit(solution)/shard_map/pallas_call | solution.py:292
  128.6 1.6 %copy.22 = f32[32,16,3,3,3]{0,1,4,3,2:T(8,128)} copy(f32[32,16,3,3,3]{0,1,4,3,2:T(8,128)} %bitcast.32) | data formatting | bytes 110592
  130.2 1.8 %copy.23 = f32[64,32,3,3,3]{0,1,4,3,2:T(8,128)} copy(f32[64,32,3,3,3]{0,1,4,3,2:T(8,128)} %bitcast.31) | data formatting | bytes 442368
Async XLA Ops:
  0.6 12.1 %copy-start.2 = (bf16[32,16,3,3,3]{0,1,4,3,2:T(8,128)(2,1)S(1)}, bf16[32,16,3,3,3]{0,1,4,3,2:T(8,128)(2,1)}, u32[]{:S(2)}) copy-start(bf16[32,16,3,3,3]{0,1,4,3,2:T(8,128)(2,1)} %param.8) | copy-start | bytes 82948
  0.6 12.7 %copy-start.1 = (bf16[64,32,3,3,3]{0,1,4,3,2:T(8,128)(2,1)S(1)}, bf16[64,32,3,3,3]{0,1,4,3,2:T(8,128)(2,1)}, u32[]{:S(2)}) copy-start(bf16[64,32,3,3,3]{0,1,4,3,2:T(8,128)(2,1)} %param.9) | copy-start | bytes 331780
  0.7 13.5 %copy-start = (bf16[1,64,16,64]{3,2,1,0:T(8,128)(2,1)S(1)}, bf16[1,64,16,64]{3,2,1,0:T(8,128)(2,1)}, u32[]{:S(2)}) copy-start(bf16[1,64,16,64]{3,2,1,0:T(8,128)(2,1)} %param.10) | copy-start | bytes 393220
  0.7 60.5 %all-to-all-start = ((bf16[32,16,2,1024]{3,2,1,0:T(2,128)(2,1)}), bf16[32,16,2,1024]{3,2,1,0:T(2,128)(2,1)S(1)}, u32[]{:S(2)}, u32[]{:S(2)}) async-start(bf16[32,16,2,1024]{3,2,1,0:T(2,128)(2,1)} %param.7), calls=%async_computation | async-start | bytes 4194304 | tf_op jit(solution)/shard_map/all_to_all | solution.py:316

commit v8 on v7

--- a/solution.py
+++ b/solution.py
@@ -148,8 +148,8 @@
     )(x, ogn, ogq, w1, w2, w2t, t1, sel2, up)
 
 
-ROUND_ORDER = ((("sample", 1),), (("space", 4),), (("sample", 2),),
-               (("space", 1), ("space", 2), ("sample", 4)), (("space", 8), ("space", 16)))
+ROUND_ORDER = ((("sample", 1),), (("space", 4),),
+               (("sample", 2), ("sample", 4), ("space", 1)), (("space", 2), ("space", 8), ("space", 16)))
 
 
 def exchange_rounds(axis_sizes):

time: 132 us -> 140 us (1.061)
  Pallas kernels: 63.6 us -> 71.3 us
    pallas_call x1, Pallas kernels: 38.8 us -> 46.5 us  [allreduce(): pl.pallas_call(functools.partial(allreduce_kernel, axis_order, rounds), o...]
where the time goes in v8:
time: 140 us
  Pallas kernels  71.3 us (51%)
  waiting for transfers between devices  44.4 us (32%)
  starting transfers between devices  12 us (9%)
  local copies, waits for them, and re-layouts  11.4 us (8%)
    pallas_call x1, Pallas kernels, allreduce(): pl.pallas_call(functools.partial(allreduce_kernel, axis_order, rounds), o...  46.5 us
    all_to_all x1, waiting for transfers between devices, body(): lax.all_to_all(crops, 'space', split_axis=0, concat_axis=2, tiled=True)  44.4 us
    pallas_call x1, Pallas kernels, per_sample(): pl.pallas_call(conv_kernel, out_shape=(jax.ShapeDtypeStruct((c2, planes2...  24.8 us
    all_to_all x1, starting transfers between devices, body(): lax.all_to_all(crops, 'space', split_axis=0, concat_axis=2, tiled=True)  12 us
    unnamed x8, local copies, waits for them, and re-layouts  3.45 us
  transfers between devices with their start and end apart: 1, of which 1 were waited for; matrix products, arithmetic and copies ran while one was open for 3% of the time, Pallas kernels for 0%

profile of v8, /device:TPU:1, one launch (start us, length us, event | category | flops | bytes accessed | tf_op | source)
XLA Modules:
  0.0 139.7 jit_solution(6617678237763883893)
XLA Ops:
  0.6 0.0 copy-start.2
  0.6 0.0 copy-start.1
  0.7 0.0 copy-start
  0.7 12.0 %all-to-all-start = ((bf16[32,16,2,1024]{3,2,1,0:T(2,128)(2,1)}), bf16[32,16,2,1024]{3,2,1,0:T(2,128)(2,1)S(1)}, u32[]{:S(2)}, u32[]{:S(2)}) async-start(bf16[32,16,2,1024]{3,2,1,0:T(2,128)(2,1)} %param.7), calls=%async_computation | async-start | bytes 4194304 | tf_op jit(solution)/shard_map/all_to_all | solution.py:316
  12.7 0.0 copy-done.2
  12.7 0.7 copy.18.w1_ref
  13.4 0.0 copy-done.1
  13.4 0.8 copy.19.w2_ref
  14.2 0.0 copy-done
  14.2 0.9 reshape_squeeze.3.ogn_ref
  15.0 0.8 copy.16
  15.8 0.2 copy.17
  15.9 0.9 reshape.31.w2t_ref
  16.8 44.4 %all-to-all-done = bf16[32,16,2,1024]{3,2,1,0:T(2,128)(2,1)S(1)} async-done(((bf16[32,16,2,1024]{3,2,1,0:T(2,128)(2,1)}), bf16[32,16,2,1024]{3,2,1,0:T(2,128)(2,1)S(1)}, u32[]{:S(2)}, u32[]{:S(2)}) %all-to-all-start) | async-done | bytes 2097184 | tf_op jit(solution)/shard_map/all_to_all | solution.py:316
  61.2 2.0 %copy.15 = bf16[1,16,32,2,1024]{4,1,3,2,0:T(8,128)(2,1)} copy(bf16[1,16,32,2,1024]{4,3,1,2,0:T(2,128)(2,1)S(1)} %bitcast.26) | data formatting | bytes 4194304 | tf_op jit(solution)/shard_map/all_to_all | solution.py:316
  63.2 24.8 %shard_map.94 = (bf16[64,1024]{1,0:T(8,128)(2,1)}, f32[32,432]{1,0:T(8,128)}, f32[64,864]{1,0:T(8,128)}) custom-call(bf16[64,16,1024]{2,1,0:T(8,128)(2,1)} %bitcast.25, bf16[64,1024]{1,0:T(8,128)(2,1)} %reshape_squeeze.3.ogn_ref, bf16[1024,64]{1,0:T(8,128)(2,1)} %bitcast.27, bf16[32,432]{1,0:T(8,128)(2,1)} %copy.18.w1_ref, bf16[64,864]{1,0:T(8,128)(2,1)} %copy.19.w2_ref, ...), custom_call_target="tpu_custom_call" | custom-call | tf_op jit(solution)/shard_map/pallas_call | solution.py:129
  88.0 1.8 %reshape.32 = bf16[1,64,16,64]{3,2,1,0:T(8,128)(2,1)} reshape(bf16[64,1024]{1,0:T(8,128)(2,1)} %get-tuple-element.8) | data formatting | bytes 262144 | tf_op jit(solution)/shard_map/reshape | solution.py:330
  89.8 46.5 %shard_map.95 = (f32[432,32]{1,0:T(8,128)}, f32[864,64]{1,0:T(8,128)}) custom-call(f32[32,432]{1,0:T(8,128)} %get-tuple-element.9.g1_ref, f32[64,864]{1,0:T(8,128)} %get-tuple-element.10.g2_ref), custom_call_target="tpu_custom_call" | custom-call | tf_op jit(solution)/shard_map/pallas_call | solution.py:292
  136.3 1.6 %copy.22 = f32[32,16,3,3,3]{0,1,4,3,2:T(8,128)} copy(f32[32,16,3,3,3]{0,1,4,3,2:T(8,128)} %bitcast.32) | data formatting | bytes 110592
  137.9 1.8 %copy.23 = f32[64,32,3,3,3]{0,1,4,3,2:T(8,128)} copy(f32[64,32,3,3,3]{0,1,4,3,2:T(8,128)} %bitcast.31) | data formatting | bytes 442368
Async XLA Ops:
  0.6 12.1 %copy-start.2 = (bf16[32,16,3,3,3]{0,1,4,3,2:T(8,128)(2,1)S(1)}, bf16[32,16,3,3,3]{0,1,4,3,2:T(8,128)(2,1)}, u32[]{:S(2)}) copy-start(bf16[32,16,3,3,3]{0,1,4,3,2:T(8,128)(2,1)} %param.8) | copy-start | bytes 82948
  0.6 12.7 %copy-start.1 = (bf16[64,32,3,3,3]{0,1,4,3,2:T(8,128)(2,1)S(1)}, bf16[64,32,3,3,3]{0,1,4,3,2:T(8,128)(2,1)}, u32[]{:S(2)}) copy-start(bf16[64,32,3,3,3]{0,1,4,3,2:T(8,128)(2,1)} %param.9) | copy-start | bytes 331780
  0.7 13.5 %copy-start = (bf16[1,64,16,64]{3,2,1,0:T(8,128)(2,1)S(1)}, bf16[1,64,16,64]{3,2,1,0:T(8,128)(2,1)}, u32[]{:S(2)}) copy-start(bf16[1,64,16,64]{3,2,1,0:T(8,128)(2,1)} %param.10) | copy-start | bytes 393220
  0.7 60.5 %all-to-all-start = ((bf16[32,16,2,1024]{3,2,1,0:T(2,128)(2,1)}), bf16[32,16,2,1024]{3,2,1,0:T(2,128)(2,1)S(1)}, u32[]{:S(2)}, u32[]{:S(2)}) async-start(bf16[32,16,2,1024]{3,2,1,0:T(2,128)(2,1)} %param.7), calls=%async_computation | async-start | bytes 4194304 | tf_op jit(solution)/shard_map/all_to_all | solution.py:316

commit v9 on v7

--- a/solution.py
+++ b/solution.py
@@ -37,9 +37,50 @@
     return t1, sel2, up
 
 
-def conv_kernel(x_ref, ogn_ref, ogq_ref, w1_ref, w2_ref, w2t_ref, t1_ref, sel2_ref, up_ref,
+def act_kernel(ogq_ref, w2t_ref, up_ref, act_ref, v_ref):
+    planes2 = v_ref.shape[0] - 1
+    c2 = v_ref.shape[2]
+    span = up_ref.shape[1] // 9
+    v_ref[planes2] = jnp.zeros(v_ref.shape[1:], v_ref.dtype)
+    for bc in range(9):
+        u = jnp.dot(ogq_ref[...], up_ref[:, bc * span:(bc + 1) * span], preferred_element_type=jnp.float32)
+        v_ref[pl.ds(0, planes2), bc] = u.astype(v_ref.dtype).reshape(planes2, c2, span)
+
+    def plane(q, carry):
+        vq = v_ref[q].reshape(9 * c2, span)
+        vq1 = v_ref[q + 1].reshape(9 * c2, span)
+        even = jnp.dot(w2t_ref[1], vq, preferred_element_type=jnp.float32)
+        odd = (jnp.dot(w2t_ref[2], vq, preferred_element_type=jnp.float32)
+               + jnp.dot(w2t_ref[0], vq1, preferred_element_type=jnp.float32))
+        act_ref[2 * q] = even.astype(act_ref.dtype)
+        act_ref[2 * q + 1] = odd.astype(act_ref.dtype)
+        return carry
+
+    lax.fori_loop(0, planes2, plane, 0)
+
+
+def act_grad_of(ogq, w2t, up):
+    c2 = w2t.shape[2] // 9
+    planes2 = ogq.shape[0] // c2
+    c1 = w2t.shape[1]
+    span = up.shape[1] // 9
+    vmem = pltpu.VMEM
+    flops = 2 * ogq.shape[0] * ogq.shape[1] * up.shape[1] + 2 * 3 * 2 * planes2 * c1 * 9 * c2 * span
+    return pl.pallas_call(
+        act_kernel,
+        out_shape=jax.ShapeDtypeStruct((2 * planes2, c1, span), jnp.bfloat16),
+        in_specs=[pl.BlockSpec(memory_space=vmem)] * 3,
+        out_specs=pl.BlockSpec(memory_space=vmem),
+        scratch_shapes=[vmem((planes2 + 1, 9, c2, span), jnp.bfloat16)],
+        compiler_params=pltpu.CompilerParams(vmem_limit_bytes=32 * 1024 * 1024),
+        cost_estimate=pl.CostEstimate(flops=flops, transcendentals=0,
+                                      bytes_accessed=2 * (ogq.size + w2t.size + up.size + 2 * planes2 * c1 * span)),
+    )(ogq, w2t, up)
+
+
+def conv_kernel(x_ref, ogn_ref, act_ref, w1_ref, w2_ref, t1_ref, sel2_ref,
                 feat_ref, fg_ref, sg_ref,
-                q1_ref, s_ref, fp_ref, a2_ref, q2_ref, s2_ref, v_ref):
+                q1_ref, s_ref, fp_ref, a2_ref, q2_ref, s2_ref):
     depth, c0, cells = x_ref.shape
     n_h = cells // 128
     c1 = w1_ref.shape[0]
@@ -47,7 +88,6 @@
     planes1 = depth // 2
     plane1 = s_ref.shape[2]
     planes2 = planes1 // 2
-    plane2 = ogq_ref.shape[1]
 
     q1_ref[0] = jnp.zeros(q1_ref.shape[1:], q1_ref.dtype)
     for h in range(n_h):
@@ -95,36 +135,23 @@
         sg_ref[...] += lax.dot_general(ogn_ref[:, n * 128:(n + 1) * 128], s2_ref[n], NT,
                                        preferred_element_type=jnp.float32)
 
-    v_ref[planes2] = jnp.zeros(v_ref.shape[1:], v_ref.dtype)
-    span = up_ref.shape[1] // 9
-    for bc in range(9):
-        u = jnp.dot(ogq_ref[...], up_ref[:, bc * span:(bc + 1) * span], preferred_element_type=jnp.float32)
-        v_ref[pl.ds(0, planes2), bc] = u.astype(v_ref.dtype).reshape(planes2, c2, span)
-
     fg_ref[...] = jnp.zeros(fg_ref.shape, fg_ref.dtype)
 
-    def back_plane(q, carry):
-        vq = v_ref[q].reshape(9 * c2, span)
-        vq1 = v_ref[q + 1].reshape(9 * c2, span)
-        even = jnp.dot(w2t_ref[1], vq, preferred_element_type=jnp.float32)
-        odd = (jnp.dot(w2t_ref[2], vq, preferred_element_type=jnp.float32)
-               + jnp.dot(w2t_ref[0], vq1, preferred_element_type=jnp.float32))
-        for k, act in ((0, even), (1, odd)):
-            d2 = 2 * q + k
-            slope = fp_ref[d2]
-            pg = (act.astype(jnp.bfloat16).astype(jnp.float32) * slope).astype(jnp.bfloat16)
-            fg_ref[...] += lax.dot_general(pg, s_ref[d2], NT, preferred_element_type=jnp.float32)
+    def back_plane(d2, carry):
+        slope = fp_ref[d2]
+        pg = (act_ref[d2].astype(jnp.float32) * slope).astype(jnp.bfloat16)
+        fg_ref[...] += lax.dot_general(pg, s_ref[d2], NT, preferred_element_type=jnp.float32)
         return carry
 
-    lax.fori_loop(0, planes2, back_plane, 0)
-
-
-def per_sample(x, ogn, ogq, w1, w2, w2t, t1, sel2, up):
+    lax.fori_loop(0, planes1, back_plane, 0)
+
+
+def per_sample(x, ogn, act, w1, w2, t1, sel2):
     depth, c0, cells = x.shape
     c1, c2 = w1.shape[0], w2.shape[0]
     planes1, planes2 = depth // 2, depth // 4
     plane1 = (HEIGHT // 2) * (WIDTH // 2)
-    plane2 = ogq.shape[1]
+    plane2 = ogn.shape[1] // planes2
     vmem = pltpu.VMEM
     return pl.pallas_call(
         conv_kernel,
@@ -133,7 +160,7 @@
             jax.ShapeDtypeStruct((c1, 27 * c0), jnp.float32),
             jax.ShapeDtypeStruct((c2, 27 * c1), jnp.float32),
         ),
-        in_specs=[pl.BlockSpec(memory_space=vmem)] * 9,
+        in_specs=[pl.BlockSpec(memory_space=vmem)] * 7,
         out_specs=[pl.BlockSpec(memory_space=vmem)] * 3,
         scratch_shapes=[
             vmem((depth + 1, c0, (cells // 128) * 384), jnp.bfloat16),
@@ -142,10 +169,9 @@
             vmem((planes1 + 1, c1, plane1), jnp.bfloat16),
             vmem((planes1 + 1, c1, 9 * 128), jnp.float32),
             vmem((planes2 // 2, 27 * c1, 128), jnp.bfloat16),
-            vmem((planes2 + 1, 9, c2, plane1), jnp.bfloat16),
         ],
         compiler_params=pltpu.CompilerParams(vmem_limit_bytes=60 * 1024 * 1024),
-    )(x, ogn, ogq, w1, w2, w2t, t1, sel2, up)
+    )(x, ogn, act, w1, w2, t1, sel2)
 
 
 ROUND_ORDER = ((("sample", 1),), (("space", 4),), (("sample", 2),),
@@ -323,10 +349,8 @@
     w2 = second_kernel.transpose(0, 2, 3, 4, 1).reshape(c2, -1)
     w2t = second_kernel.transpose(2, 1, 3, 4, 0).reshape(3, c1, -1)
     t1, sel2, up = selection_tables(WIDTH, HEIGHT // 2, WIDTH // 2)
-    feat, fg, sg = per_sample(
-        x, ogn, ogq, w1, w2, w2t,
-        jnp.asarray(t1, jnp.bfloat16), jnp.asarray(sel2, jnp.bfloat16), jnp.asarray(up, jnp.bfloat16),
-    )
+    act = act_grad_of(ogq, w2t, jnp.asarray(up, jnp.bfloat16))
+    feat, fg, sg = per_sample(x, ogn, act, w1, w2, jnp.asarray(t1, jnp.bfloat16), jnp.asarray(sel2, jnp.bfloat16))
     features_out = feat.reshape(out_grad.shape)
     fg, sg = allreduce(fg, sg, axis_order, axis_sizes)
     first_grad = fg.reshape(3, 3, 3, channels_in, c1).transpose(4, 3, 0, 1, 2)

time: 132 us -> 130 us (0.985)
  waiting for transfers between devices: 44.4 us -> 39.3 us
  Pallas kernels: 63.6 us -> 66.9 us
    pallas_call x0 -> x1, Pallas kernels: none -> 5.5 us  [act_grad_of(): pl.pallas_call(act_kernel, out_shape=jax.ShapeDtypeStruct((2 * planes2, c...]
    all_to_all x1, waiting for transfers between devices: 44.4 us -> 39.3 us  [body(): lax.all_to_all(crops, 'space', split_axis=0, concat_axis=2, tiled=True)]
    pallas_call x1, Pallas kernels: 24.8 us -> 22.6 us  [per_sample(): pl.pallas_call(conv_kernel, out_shape=(jax.ShapeDtypeStruct((c2, planes2...]
    unnamed x8 -> x12, local copies, waits for them, and re-layouts: 3.45 us -> 4.26 us
  transfers between devices with their start and end apart: 1 -> 1, of which waited for: 1 -> 1; matrix products, arithmetic and copies ran while one was open for 3% -> 2% of each run, Pallas kernels for 0% -> 4%
where the time goes in v9:
time: 130 us
  Pallas kernels  66.9 us (51%)
  waiting for transfers between devices  39.3 us (30%)
  starting transfers between devices  12 us (9%)
  local copies, waits for them, and re-layouts  10.9 us (8%)
    all_to_all x1, waiting for transfers between devices, body(): lax.all_to_all(crops, 'space', split_axis=0, concat_axis=2, tiled=True)  39.3 us
    pallas_call x1, Pallas kernels, allreduce(): pl.pallas_call(functools.partial(allreduce_kernel, axis_order, rounds), o...  38.8 us
    pallas_call x1, Pallas kernels, per_sample(): pl.pallas_call(conv_kernel, out_shape=(jax.ShapeDtypeStruct((c2, planes2...  22.6 us
    all_to_all x1, starting transfers between devices, body(): lax.all_to_all(crops, 'space', split_axis=0, concat_axis=2, tiled=True)  12 us
    pallas_call x1, Pallas kernels, act_grad_of(): pl.pallas_call(act_kernel, out_shape=jax.ShapeDtypeStruct((2 * planes2, c...  5.5 us
    unnamed x12, local copies, waits for them, and re-layouts  4.26 us
  transfers between devices with their start and end apart: 1, of which 1 were waited for; matrix products, arithmetic and copies ran while one was open for 2% of the time, Pallas kernels for 4%

profile of v9, /device:TPU:1, one launch (start us, length us, event | category | flops | bytes accessed | tf_op | source)
XLA Modules:
  0.0 129.9 jit_solution(9938899258386754332)
XLA Ops:
  0.6 0.0 copy-start.4
  0.6 0.0 copy-start.3
  0.7 0.0 copy-start.2
  0.7 12.0 %all-to-all-start = ((bf16[32,16,2,1024]{3,2,1,0:T(2,128)(2,1)}), bf16[32,16,2,1024]{3,2,1,0:T(2,128)(2,1)S(1)}, u32[]{:S(2)}, u32[]{:S(2)}) async-start(bf16[32,16,2,1024]{3,2,1,0:T(2,128)(2,1)} %param.7), calls=%async_computation | async-start | bytes 4194304 | tf_op jit(solution)/shard_map/all_to_all | solution.py:342
  12.7 0.0 copy-start.1
  12.7 0.0 copy-done.4
  12.7 0.7 copy.18.w1_ref
  13.4 0.0 copy-done.3
  13.4 0.8 copy.19.w2_ref
  14.2 0.0 copy-done.2
  14.2 0.9 reshape_squeeze.3.ogn_ref
  15.0 0.1 copy.16
  15.1 0.2 copy.17
  15.3 0.2 reshape.29.w2t_ref
  15.5 0.0 copy-done.1
  15.5 5.5 %shard_map.94.act_ref = bf16[32,32,256]{2,1,0:T(8,128)(2,1)S(1)} custom-call(bf16[1024,64]{1,0:T(8,128)(2,1)S(1)} %bitcast.25, bf16[3,32,576]{2,1,0:T(8,128)(2,1)S(1)} %reshape.29.w2t_ref, bf16[64,2304]{1,0:T(8,128)(2,1)S(1)} %copy-done.1), custom_call_target="tpu_custom_call" | custom-call | flops 1207959552 | bytes 1060864 | tf_op jit(solution)/shard_map/pallas_call | solution.py:69
  21.0 0.0 copy-start
  21.0 0.8 copy-done
  21.8 39.3 %all-to-all-done = bf16[32,16,2,1024]{3,2,1,0:T(2,128)(2,1)S(1)} async-done(((bf16[32,16,2,1024]{3,2,1,0:T(2,128)(2,1)}), bf16[32,16,2,1024]{3,2,1,0:T(2,128)(2,1)S(1)}, u32[]{:S(2)}, u32[]{:S(2)}) %all-to-all-start) | async-done | bytes 2097184 | tf_op jit(solution)/shard_map/all_to_all | solution.py:342
  61.2 2.0 %copy.15 = bf16[1,16,32,2,1024]{4,1,3,2,0:T(8,128)(2,1)} copy(bf16[1,16,32,2,1024]{4,3,1,2,0:T(2,128)(2,1)S(1)} %bitcast.27) | data formatting | bytes 4194304 | tf_op jit(solution)/shard_map/all_to_all | solution.py:342
  63.2 22.6 %shard_map.95 = (bf16[64,1024]{1,0:T(8,128)(2,1)}, f32[32,432]{1,0:T(8,128)}, f32[64,864]{1,0:T(8,128)}) custom-call(bf16[64,16,1024]{2,1,0:T(8,128)(2,1)} %bitcast.26, bf16[64,1024]{1,0:T(8,128)(2,1)} %reshape_squeeze.3.ogn_ref, bf16[32,32,256]{2,1,0:T(8,128)(2,1)} %copy-done, bf16[32,432]{1,0:T(8,128)(2,1)} %copy.18.w1_ref, bf16[64,864]{1,0:T(8,128)(2,1)} %copy.19.w2_ref, ...), custom_call_target="tpu_custom_call" | custom-call | tf_op jit(solution)/shard_map/pallas_call | solution.py:156
  85.8 1.8 %reshape.32 = bf16[1,64,16,64]{3,2,1,0:T(8,128)(2,1)} reshape(bf16[64,1024]{1,0:T(8,128)(2,1)} %get-tuple-element.8) | data formatting | bytes 262144 | tf_op jit(solution)/shard_map/reshape | solution.py:354
  87.6 38.8 %shard_map.96 = (f32[432,32]{1,0:T(8,128)}, f32[864,64]{1,0:T(8,128)}) custom-call(f32[32,432]{1,0:T(8,128)} %get-tuple-element.9.g1_ref, f32[64,864]{1,0:T(8,128)} %get-tuple-element.10.g2_ref), custom_call_target="tpu_custom_call" | custom-call | tf_op jit(solution)/shard_map/pallas_call | solution.py:318
  126.4 1.6 %copy.22 = f32[32,16,3,3,3]{0,1,4,3,2:T(8,128)} copy(f32[32,16,3,3,3]{0,1,4,3,2:T(8,128)} %bitcast.32) | data formatting | bytes 110592
  128.1 1.8 %copy.23 = f32[64,32,3,3,3]{0,1,4,3,2:T(8,128)} copy(f32[64,32,3,3,3]{0,1,4,3,2:T(8,128)} %bitcast.31) | data formatting | bytes 442368
Async XLA Ops:
  0.6 12.1 %copy-start.4 = (bf16[32,16,3,3,3]{0,1,4,3,2:T(8,128)(2,1)S(1)}, bf16[32,16,3,3,3]{0,1,4,3,2:T(8,128)(2,1)}, u32[]{:S(2)}) copy-start(bf16[32,16,3,3,3]{0,1,4,3,2:T(8,128)(2,1)} %param.8) | copy-start | bytes 82948
  0.6 12.8 %copy-start.3 = (bf16[64,32,3,3,3]{0,1,4,3,2:T(8,128)(2,1)S(1)}, bf16[64,32,3,3,3]{0,1,4,3,2:T(8,128)(2,1)}, u32[]{:S(2)}) copy-start(bf16[64,32,3,3,3]{0,1,4,3,2:T(8,128)(2,1)} %param.9) | copy-start | bytes 331780
  0.7 13.5 %copy-start.2 = (bf16[1,64,16,64]{3,2,1,0:T(8,128)(2,1)S(1)}, bf16[1,64,16,64]{3,2,1,0:T(8,128)(2,1)}, u32[]{:S(2)}) copy-start(bf16[1,64,16,64]{3,2,1,0:T(8,128)(2,1)} %param.10) | copy-start | bytes 393220
  0.7 60.5 %all-to-all-start = ((bf16[32,16,2,1024]{3,2,1,0:T(2,128)(2,1)}), bf16[32,16,2,1024]{3,2,1,0:T(2,128)(2,1)S(1)}, u32[]{:S(2)}, u32[]{:S(2)}) async-start(bf16[32,16,2,1024]{3,2,1,0:T(2,128)(2,1)} %param.7), calls=%async_computation | async-start | bytes 4194304 | tf_op jit(solution)/shard_map/all_to_all | solution.py:342
  12.7 2.8 %copy-start.1 = (bf16[64,2304]{1,0:T(8,128)(2,1)S(1)}, bf16[64,2304]{1,0:T(8,128)(2,1)}, u32[]{:S(2)}) copy-start(bf16[64,2304]{1,0:T(8,128)(2,1)} %constant.6.clone.up_ref) | copy-start | bytes 884740
  21.0 0.8 copy-start

commit v10 on v9

--- a/solution.py
+++ b/solution.py
@@ -225,13 +225,34 @@
             members.append((t, slot, tuple(there[a] for a in axis_order)))
         plan_rounds.append((group, own, members))
 
-    barrier = pltpu.get_barrier_semaphore()
-    count = 0
+    def group_members(group):
+        own = sum(bit_of(axis, bit) * 2 ** idx for idx, (axis, bit) in enumerate(group))
+        members = []
+        for t in range(1, 2 ** len(group)):
+            there = dict(me)
+            slot = 0
+            flips = []
+            for idx, (axis, bit) in enumerate(group):
+                flip = (t // 2 ** idx) % 2
+                if flip:
+                    there[axis] = there[axis] + bit - 2 * bit * bit_of(axis, bit)
+                    flips.append((axis, bit))
+                slot = slot + ((bit_of(axis, bit) + flip) % 2) * 2 ** idx
+            members.append((t, slot, tuple(there[a] for a in axis_order), frozenset(flips), flips))
+        return own, members
+
+    halving_bits = [rounds[r][0] for r in range(max(halvings(acc.shape[0], rounds) for acc in (o1_ref, o2_ref)))]
+    seen = {}
     for group, own, members in plan_rounds:
         for t, slot, device in members:
-            pl.semaphore_signal(barrier, 1, device_id=device, device_id_type=pl.DeviceIdType.MESH)
-            count += 1
-    pl.semaphore_wait(barrier, count)
+            flips = frozenset((axis, bit) for idx, (axis, bit) in enumerate(group) if (t // 2 ** idx) % 2)
+            seen[flips] = device
+    for t, slot, device, flips, _ in group_members(halving_bits)[1]:
+        seen[flips] = device
+    barrier = pltpu.get_barrier_semaphore()
+    for device in seen.values():
+        pl.semaphore_signal(barrier, 1, device_id=device, device_id_type=pl.DeviceIdType.MESH)
+    pl.semaphore_wait(barrier, len(seen))
 
     accs = (o1_ref, o2_ref)
     recvs = (r1_ref, r2_ref)
@@ -289,22 +310,31 @@
                     total = total + xbuf[slot_r, q]
                 acc[pl.ds(off, rows)] = total
 
-    for r in reversed(range(len(plan_rounds))):
-        copies, places = [], []
-        group, own, members = plan_rounds[r]
-        for k, (acc, gather, plan) in enumerate(zip(accs, gathers, plans)):
-            for step, keep, give, half in plan["kept"]:
-                if step == r:
-                    t, slot, device = members[0]
-                    copies.append(remote(acc.at[pl.ds(keep, half)], gather.at[r, pl.ds(0, half)],
-                                         gather_sem.at[r, 0, k], gather_sem.at[r, 1, k], device))
-                    places.append((acc, gather, give, half))
-        for copy in copies:
-            copy.start()
-        for copy in copies:
-            copy.wait()
-        for acc, gather, give, half in places:
-            acc[pl.ds(give, half)] = gather[r, pl.ds(0, half)]
+    copies, places = [], []
+    for k, (acc, gather, plan) in enumerate(zip(accs, gathers, plans)):
+        if plan["h"] == 0:
+            continue
+        bits = [rounds[r][0] for r in range(plan["h"])]
+        halves = [half for step, keep, give, half in plan["kept"]]
+        own, members = group_members(bits)
+        rows, off = plan["rows"], plan["off"]
+        for t, slot, device, flips, flip_list in members:
+            copies.append((
+                remote(acc.at[pl.ds(off, rows)], gather.at[own], gather_sem.at[t, 0, k], gather_sem.at[own, 1, k], device),
+                remote(acc.at[pl.ds(off, rows)], gather.at[slot], gather_sem.at[t, 0, k], gather_sem.at[slot, 1, k], device)))
+            where = 0
+            for idx, (axis, bit) in enumerate(bits):
+                flip = 1 if (axis, bit) in flips else 0
+                where = where + ((bit_of(axis, bit) + flip) % 2) * halves[idx]
+            places.append((acc, gather, slot, pl.multiple_of(where, 8), rows))
+    for send, recv in copies:
+        send.start()
+    for send, recv in copies:
+        send.wait_send()
+    for send, recv in copies:
+        recv.wait_recv()
+    for acc, gather, slot, where, rows in places:
+        acc[pl.ds(where, rows)] = gather[slot]
     t1_ref[...] = o1_ref[...].T
     t2_ref[...] = o2_ref[...].T
 
@@ -315,6 +345,7 @@
     width = max(2 ** len(group) for group in rounds)
     vmem = pltpu.VMEM
     chunk = [g.shape[0] // 2 ** halvings(g.shape[0], rounds) for g in (g1, g2)]
+    gwidth = max(2 ** halvings(g.shape[0], rounds) for g in (g1, g2))
     return pl.pallas_call(
         functools.partial(allreduce_kernel, axis_order, rounds),
         out_shape=(jax.ShapeDtypeStruct(g1.shape[::-1], g1.dtype), jax.ShapeDtypeStruct(g2.shape[::-1], g2.dtype)),
@@ -325,13 +356,13 @@
             vmem(g2.shape, g2.dtype),
             vmem((n, g1.shape[0] // 2) + g1.shape[1:], g1.dtype),
             vmem((n, g2.shape[0] // 2) + g2.shape[1:], g2.dtype),
-            vmem((n, g1.shape[0] // 2) + g1.shape[1:], g1.dtype),
-            vmem((n, g2.shape[0] // 2) + g2.shape[1:], g2.dtype),
+            vmem((gwidth, chunk[0]) + g1.shape[1:], g1.dtype),
+            vmem((gwidth, chunk[1]) + g2.shape[1:], g2.dtype),
             vmem((n, width, chunk[0]) + g1.shape[1:], g1.dtype),
             vmem((n, width, chunk[1]) + g2.shape[1:], g2.dtype),
             pltpu.SemaphoreType.DMA((n, width, 2)),
             pltpu.SemaphoreType.DMA((n, width, 2)),
-            pltpu.SemaphoreType.DMA((n, 2, 2)),
+            pltpu.SemaphoreType.DMA((gwidth, 2, 2)),
         ],
         compiler_params=pltpu.CompilerParams(collective_id=0, has_side_effects=True),
     )(g1, g2)

time: 130 us -> 128 us (0.985)
  Pallas kernels: 66.9 us -> 64.6 us
    pallas_call x1, Pallas kernels: 38.8 us -> 36.5 us  [allreduce(): pl.pallas_call(functools.partial(allreduce_kernel, axis_order, rounds), o...]
where the time goes in v10:
time: 128 us
  Pallas kernels  64.6 us (50%)
  waiting for transfers between devices  39.3 us (31%)
  starting transfers between devices  12 us (9%)
  local copies, waits for them, and re-layouts  10.9 us (9%)
    all_to_all x1, waiting for transfers between devices, body(): lax.all_to_all(crops, 'space', split_axis=0, concat_axis=2, tiled=True)  39.3 us
    pallas_call x1, Pallas kernels, allreduce(): pl.pallas_call(functools.partial(allreduce_kernel, axis_order, rounds), o...  36.5 us
    pallas_call x1, Pallas kernels, per_sample(): pl.pallas_call(conv_kernel, out_shape=(jax.ShapeDtypeStruct((c2, planes2...  22.6 us
    all_to_all x1, starting transfers between devices, body(): lax.all_to_all(crops, 'space', split_axis=0, concat_axis=2, tiled=True)  12 us
    pallas_call x1, Pallas kernels, act_grad_of(): pl.pallas_call(act_kernel, out_shape=jax.ShapeDtypeStruct((2 * planes2, c...  5.5 us
    unnamed x12, local copies, waits for them, and re-layouts  4.26 us
  transfers between devices with their start and end apart: 1, of which 1 were waited for; matrix products, arithmetic and copies ran while one was open for 2% of the time, Pallas kernels for 4%

profile of v10, /device:TPU:1, one launch (start us, length us, event | category | flops | bytes accessed | tf_op | source)
XLA Modules:
  0.0 127.6 jit_solution(5630318944207661006)
XLA Ops:
  0.6 0.0 copy-start.4
  0.6 0.0 copy-start.3
  0.7 0.0 copy-start.2
  0.7 12.0 %all-to-all-start = ((bf16[32,16,2,1024]{3,2,1,0:T(2,128)(2,1)}), bf16[32,16,2,1024]{3,2,1,0:T(2,128)(2,1)S(1)}, u32[]{:S(2)}, u32[]{:S(2)}) async-start(bf16[32,16,2,1024]{3,2,1,0:T(2,128)(2,1)} %param.7), calls=%async_computation | async-start | bytes 4194304 | tf_op jit(solution)/shard_map/all_to_all | solution.py:373
  12.7 0.0 copy-start.1
  12.7 0.0 copy-done.4
  12.7 0.7 copy.18.w1_ref
  13.4 0.0 copy-done.3
  13.4 0.8 copy.19.w2_ref
  14.2 0.0 copy-done.2
  14.2 0.9 reshape_squeeze.3.ogn_ref
  15.0 0.1 copy.16
  15.1 0.2 copy.17
  15.3 0.2 reshape.29.w2t_ref
  15.5 0.0 copy-done.1
  15.5 5.5 %shard_map.94.act_ref = bf16[32,32,256]{2,1,0:T(8,128)(2,1)S(1)} custom-call(bf16[1024,64]{1,0:T(8,128)(2,1)S(1)} %bitcast.25, bf16[3,32,576]{2,1,0:T(8,128)(2,1)S(1)} %reshape.29.w2t_ref, bf16[64,2304]{1,0:T(8,128)(2,1)S(1)} %copy-done.1), custom_call_target="tpu_custom_call" | custom-call | flops 1207959552 | bytes 1060864 | tf_op jit(solution)/shard_map/pallas_call | solution.py:69
  21.0 0.0 copy-start
  21.0 0.8 copy-done
  21.8 39.3 %all-to-all-done = bf16[32,16,2,1024]{3,2,1,0:T(2,128)(2,1)S(1)} async-done(((bf16[32,16,2,1024]{3,2,1,0:T(2,128)(2,1)}), bf16[32,16,2,1024]{3,2,1,0:T(2,128)(2,1)S(1)}, u32[]{:S(2)}, u32[]{:S(2)}) %all-to-all-start) | async-done | bytes 2097184 | tf_op jit(solution)/shard_map/all_to_all | solution.py:373
  61.2 2.0 %copy.15 = bf16[1,16,32,2,1024]{4,1,3,2,0:T(8,128)(2,1)} copy(bf16[1,16,32,2,1024]{4,3,1,2,0:T(2,128)(2,1)S(1)} %bitcast.27) | data formatting | bytes 4194304 | tf_op jit(solution)/shard_map/all_to_all | solution.py:373
  63.2 22.6 %shard_map.95 = (bf16[64,1024]{1,0:T(8,128)(2,1)}, f32[32,432]{1,0:T(8,128)}, f32[64,864]{1,0:T(8,128)}) custom-call(bf16[64,16,1024]{2,1,0:T(8,128)(2,1)} %bitcast.26, bf16[64,1024]{1,0:T(8,128)(2,1)} %reshape_squeeze.3.ogn_ref, bf16[32,32,256]{2,1,0:T(8,128)(2,1)} %copy-done, bf16[32,432]{1,0:T(8,128)(2,1)} %copy.18.w1_ref, bf16[64,864]{1,0:T(8,128)(2,1)} %copy.19.w2_ref, ...), custom_call_target="tpu_custom_call" | custom-call | tf_op jit(solution)/shard_map/pallas_call | solution.py:156
  85.8 1.8 %reshape.32 = bf16[1,64,16,64]{3,2,1,0:T(8,128)(2,1)} reshape(bf16[64,1024]{1,0:T(8,128)(2,1)} %get-tuple-element.8) | data formatting | bytes 262144 | tf_op jit(solution)/shard_map/reshape | solution.py:385
  87.6 36.5 %shard_map.96 = (f32[432,32]{1,0:T(8,128)}, f32[864,64]{1,0:T(8,128)}) custom-call(f32[32,432]{1,0:T(8,128)} %get-tuple-element.9.g1_ref, f32[64,864]{1,0:T(8,128)} %get-tuple-element.10.g2_ref), custom_call_target="tpu_custom_call" | custom-call | tf_op jit(solution)/shard_map/pallas_call | solution.py:349
  124.1 1.6 %copy.22 = f32[32,16,3,3,3]{0,1,4,3,2:T(8,128)} copy(f32[32,16,3,3,3]{0,1,4,3,2:T(8,128)} %bitcast.32) | data formatting | bytes 110592
  125.8 1.8 %copy.23 = f32[64,32,3,3,3]{0,1,4,3,2:T(8,128)} copy(f32[64,32,3,3,3]{0,1,4,3,2:T(8,128)} %bitcast.31) | data formatting | bytes 442368
Async XLA Ops:
  0.6 12.1 %copy-start.4 = (bf16[32,16,3,3,3]{0,1,4,3,2:T(8,128)(2,1)S(1)}, bf16[32,16,3,3,3]{0,1,4,3,2:T(8,128)(2,1)}, u32[]{:S(2)}) copy-start(bf16[32,16,3,3,3]{0,1,4,3,2:T(8,128)(2,1)} %param.8) | copy-start | bytes 82948
  0.6 12.8 %copy-start.3 = (bf16[64,32,3,3,3]{0,1,4,3,2:T(8,128)(2,1)S(1)}, bf16[64,32,3,3,3]{0,1,4,3,2:T(8,128)(2,1)}, u32[]{:S(2)}) copy-start(bf16[64,32,3,3,3]{0,1,4,3,2:T(8,128)(2,1)} %param.9) | copy-start | bytes 331780
  0.7 13.5 %copy-start.2 = (bf16[1,64,16,64]{3,2,1,0:T(8,128)(2,1)S(1)}, bf16[1,64,16,64]{3,2,1,0:T(8,128)(2,1)}, u32[]{:S(2)}) copy-start(bf16[1,64,16,64]{3,2,1,0:T(8,128)(2,1)} %param.10) | copy-start | bytes 393220
  0.7 60.5 %all-to-all-start = ((bf16[32,16,2,1024]{3,2,1,0:T(2,128)(2,1)}), bf16[32,16,2,1024]{3,2,1,0:T(2,128)(2,1)S(1)}, u32[]{:S(2)}, u32[]{:S(2)}) async-start(bf16[32,16,2,1024]{3,2,1,0:T(2,128)(2,1)} %param.7), calls=%async_computation | async-start | bytes 4194304 | tf_op jit(solution)/shard_map/all_to_all | solution.py:373
  12.7 2.8 %copy-start.1 = (bf16[64,2304]{1,0:T(8,128)(2,1)S(1)}, bf16[64,2304]{1,0:T(8,128)(2,1)}, u32[]{:S(2)}) copy-start(bf16[64,2304]{1,0:T(8,128)(2,1)} %constant.6.clone.up_ref) | copy-start | bytes 884740
  21.0 0.8 copy-start

commit v11 on v10

--- a/solution.py
+++ b/solution.py
@@ -131,7 +131,9 @@
                 hi = q2_ref[4 * n + a + 2, :, bc * 128:(bc + 1) * 128]
                 s2_ref[n, r0:r0 + c1, :] = (lo + pltpu.roll(hi, 64, 1)).astype(s2_ref.dtype)
         feat = jnp.dot(w2_ref[...], s2_ref[n], preferred_element_type=jnp.float32)
-        feat_ref[:, n * 128:(n + 1) * 128] = feat.astype(feat_ref.dtype)
+        half = feat_ref.shape[2]
+        feat_ref[:, 2 * n, :] = feat[:, :half].astype(feat_ref.dtype)
+        feat_ref[:, 2 * n + 1, :] = feat[:, half:].astype(feat_ref.dtype)
         sg_ref[...] += lax.dot_general(ogn_ref[:, n * 128:(n + 1) * 128], s2_ref[n], NT,
                                        preferred_element_type=jnp.float32)
 
@@ -156,7 +158,7 @@
     return pl.pallas_call(
         conv_kernel,
         out_shape=(
-            jax.ShapeDtypeStruct((c2, planes2 * plane2), jnp.bfloat16),
+            jax.ShapeDtypeStruct((c2, planes2, plane2), jnp.bfloat16),
             jax.ShapeDtypeStruct((c1, 27 * c0), jnp.float32),
             jax.ShapeDtypeStruct((c2, 27 * c1), jnp.float32),
         ),

time: 128 us -> 126 us (0.984)
  local copies, waits for them, and re-layouts: 10.9 us -> 9.05 us
    reshape x1 -> x0, local copies, waits for them, and re-layouts: 1.82 us -> none  [body(): features_out = feat.reshape(out_grad.shape)]
where the time goes in v11:
time: 126 us
  Pallas kernels  64.8 us (51%)
  waiting for transfers between devices  39.3 us (31%)
  starting transfers between devices  12 us (10%)
  local copies, waits for them, and re-layouts  9.05 us (7%)
    all_to_all x1, waiting for transfers between devices, body(): lax.all_to_all(crops, 'space', split_axis=0, concat_axis=2, tiled=True)  39.3 us
    pallas_call x1, Pallas kernels, allreduce(): pl.pallas_call(functools.partial(allreduce_kernel, axis_order, rounds), o...  36.5 us
    pallas_call x1, Pallas kernels, per_sample(): pl.pallas_call(conv_kernel, out_shape=(jax.ShapeDtypeStruct((c2, planes2,...  22.8 us
    all_to_all x1, starting transfers between devices, body(): lax.all_to_all(crops, 'space', split_axis=0, concat_axis=2, tiled=True)  12 us
    pallas_call x1, Pallas kernels, act_grad_of(): pl.pallas_call(act_kernel, out_shape=jax.ShapeDtypeStruct((2 * planes2, c...  5.5 us
    unnamed x12, local copies, waits for them, and re-layouts  4.26 us
  transfers between devices with their start and end apart: 1, of which 1 were waited for; matrix products, arithmetic and copies ran while one was open for 2% of the time, Pallas kernels for 4%

profile of v11, /device:TPU:1, one launch (start us, length us, event | category | flops | bytes accessed | tf_op | source)
XLA Modules:
  0.0 126.0 jit_solution(11941467721354518797)
XLA Ops:
  0.6 0.0 copy-start.4
  0.6 0.0 copy-start.3
  0.7 0.0 copy-start.2
  0.7 12.0 %all-to-all-start = ((bf16[32,16,2,1024]{3,2,1,0:T(2,128)(2,1)}), bf16[32,16,2,1024]{3,2,1,0:T(2,128)(2,1)S(1)}, u32[]{:S(2)}, u32[]{:S(2)}) async-start(bf16[32,16,2,1024]{3,2,1,0:T(2,128)(2,1)} %param.7), calls=%async_computation | async-start | bytes 4194304 | tf_op jit(solution)/shard_map/all_to_all | solution.py:375
  12.7 0.0 copy-start.1
  12.7 0.0 copy-done.4
  12.7 0.7 copy.18.w1_ref
  13.4 0.0 copy-done.3
  13.4 0.8 copy.19.w2_ref
  14.2 0.0 copy-done.2
  14.2 0.9 reshape_squeeze.3.ogn_ref
  15.0 0.1 copy.16
  15.1 0.2 copy.17
  15.3 0.2 reshape.29.w2t_ref
  15.5 0.0 copy-done.1
  15.5 5.5 %shard_map.94.act_ref = bf16[32,32,256]{2,1,0:T(8,128)(2,1)S(1)} custom-call(bf16[1024,64]{1,0:T(8,128)(2,1)S(1)} %bitcast.26, bf16[3,32,576]{2,1,0:T(8,128)(2,1)S(1)} %reshape.29.w2t_ref, bf16[64,2304]{1,0:T(8,128)(2,1)S(1)} %copy-done.1), custom_call_target="tpu_custom_call" | custom-call | flops 1207959552 | bytes 1060864 | tf_op jit(solution)/shard_map/pallas_call | solution.py:69
  21.0 0.0 copy-start
  21.0 0.8 copy-done
  21.8 39.3 %all-to-all-done = bf16[32,16,2,1024]{3,2,1,0:T(2,128)(2,1)S(1)} async-done(((bf16[32,16,2,1024]{3,2,1,0:T(2,128)(2,1)}), bf16[32,16,2,1024]{3,2,1,0:T(2,128)(2,1)S(1)}, u32[]{:S(2)}, u32[]{:S(2)}) %all-to-all-start) | async-done | bytes 2097184 | tf_op jit(solution)/shard_map/all_to_all | solution.py:375
  61.2 2.0 %copy.15 = bf16[1,16,32,2,1024]{4,1,3,2,0:T(8,128)(2,1)} copy(bf16[1,16,32,2,1024]{4,3,1,2,0:T(2,128)(2,1)S(1)} %bitcast.28) | data formatting | bytes 4194304 | tf_op jit(solution)/shard_map/all_to_all | solution.py:375
  63.2 22.8 %shard_map.95 = (bf16[64,16,64]{2,1,0:T(8,128)(2,1)}, f32[32,432]{1,0:T(8,128)}, f32[64,864]{1,0:T(8,128)}) custom-call(bf16[64,16,1024]{2,1,0:T(8,128)(2,1)} %bitcast.27, bf16[64,1024]{1,0:T(8,128)(2,1)} %reshape_squeeze.3.ogn_ref, bf16[32,32,256]{2,1,0:T(8,128)(2,1)} %copy-done, bf16[32,432]{1,0:T(8,128)(2,1)} %copy.18.w1_ref, ...), custom_call_target="tpu_custom_call" | custom-call | tf_op jit(solution)/shard_map/pallas_call | solution.py:158
  86.0 36.5 %shard_map.96 = (f32[432,32]{1,0:T(8,128)}, f32[864,64]{1,0:T(8,128)}) custom-call(f32[32,432]{1,0:T(8,128)} %get-tuple-element.9.g1_ref, f32[64,864]{1,0:T(8,128)} %get-tuple-element.10.g2_ref), custom_call_target="tpu_custom_call" | custom-call | tf_op jit(solution)/shard_map/pallas_call | solution.py:351
  122.5 1.6 %copy.22 = f32[32,16,3,3,3]{0,1,4,3,2:T(8,128)} copy(f32[32,16,3,3,3]{0,1,4,3,2:T(8,128)} %bitcast.33) | data formatting | bytes 110592
  124.2 1.8 %copy.23 = f32[64,32,3,3,3]{0,1,4,3,2:T(8,128)} copy(f32[64,32,3,3,3]{0,1,4,3,2:T(8,128)} %bitcast.32) | data formatting | bytes 442368
Async XLA Ops:
  0.6 12.1 %copy-start.4 = (bf16[32,16,3,3,3]{0,1,4,3,2:T(8,128)(2,1)S(1)}, bf16[32,16,3,3,3]{0,1,4,3,2:T(8,128)(2,1)}, u32[]{:S(2)}) copy-start(bf16[32,16,3,3,3]{0,1,4,3,2:T(8,128)(2,1)} %param.8) | copy-start | bytes 82948
  0.6 12.8 %copy-start.3 = (bf16[64,32,3,3,3]{0,1,4,3,2:T(8,128)(2,1)S(1)}, bf16[64,32,3,3,3]{0,1,4,3,2:T(8,128)(2,1)}, u32[]{:S(2)}) copy-start(bf16[64,32,3,3,3]{0,1,4,3,2:T(8,128)(2,1)} %param.9) | copy-start | bytes 331780
  0.7 13.5 %copy-start.2 = (bf16[1,64,16,64]{3,2,1,0:T(8,128)(2,1)S(1)}, bf16[1,64,16,64]{3,2,1,0:T(8,128)(2,1)}, u32[]{:S(2)}) copy-start(bf16[1,64,16,64]{3,2,1,0:T(8,128)(2,1)} %param.10) | copy-start | bytes 393220
  0.7 60.5 %all-to-all-start = ((bf16[32,16,2,1024]{3,2,1,0:T(2,128)(2,1)}), bf16[32,16,2,1024]{3,2,1,0:T(2,128)(2,1)S(1)}, u32[]{:S(2)}, u32[]{:S(2)}) async-start(bf16[32,16,2,1024]{3,2,1,0:T(2,128)(2,1)} %param.7), calls=%async_computation | async-start | bytes 4194304 | tf_op jit(solution)/shard_map/all_to_all | solution.py:375
  12.7 2.8 %copy-start.1 = (bf16[64,2304]{1,0:T(8,128)(2,1)S(1)}, bf16[64,2304]{1,0:T(8,128)(2,1)}, u32[]{:S(2)}) copy-start(bf16[64,2304]{1,0:T(8,128)(2,1)} %constant.6.clone.up_ref) | copy-start | bytes 884740
  21.0 0.8 copy-start

commit v12 on v11

--- a/solution.py
+++ b/solution.py
@@ -115,7 +115,7 @@
         a2_ref[pd + 1] = (pre * sig).astype(a2_ref.dtype)
         return carry
 
-    lax.fori_loop(0, planes1, build_plane, 0)
+    lax.fori_loop(0, planes1, build_plane, 0, unroll=4)
 
     a2 = a2_ref[...].reshape((planes1 + 1) * c1, plane1)
     for bc in range(9):
@@ -145,7 +145,7 @@
         fg_ref[...] += lax.dot_general(pg, s_ref[d2], NT, preferred_element_type=jnp.float32)
         return carry
 
-    lax.fori_loop(0, planes1, back_plane, 0)
+    lax.fori_loop(0, planes1, back_plane, 0, unroll=8)
 
 
 def per_sample(x, ogn, act, w1, w2, t1, sel2):

time: 126 us -> 118 us (0.937)
  Pallas kernels: 64.8 us -> 56.2 us
    pallas_call x1, Pallas kernels: 22.8 us -> 14.2 us  [per_sample(): pl.pallas_call(conv_kernel, out_shape=(jax.ShapeDtypeStruct((c2, planes2,...]
  transfers between devices with their start and end apart: 1 -> 1, of which waited for: 1 -> 1; matrix products, arithmetic and copies ran while one was open for 2% -> 2% of each run, Pallas kernels for 4% -> 5%
where the time goes in v12:
time: 118 us; the launch traced here: 117 us
  Pallas kernels  56.2 us (48%)
  waiting for transfers between devices  39.3 us (33%)
  starting transfers between devices  12 us (10%)
  local copies, waits for them, and re-layouts  9.05 us (8%)
    all_to_all x1, waiting for transfers between devices, body(): lax.all_to_all(crops, 'space', split_axis=0, concat_axis=2, tiled=True)  39.3 us
    pallas_call x1, Pallas kernels, allreduce(): pl.pallas_call(functools.partial(allreduce_kernel, axis_order, rounds), o...  36.5 us
    pallas_call x1, Pallas kernels, per_sample(): pl.pallas_call(conv_kernel, out_shape=(jax.ShapeDtypeStruct((c2, planes2,...  14.2 us
    all_to_all x1, starting transfers between devices, body(): lax.all_to_all(crops, 'space', split_axis=0, concat_axis=2, tiled=True)  12 us
    pallas_call x1, Pallas kernels, act_grad_of(): pl.pallas_call(act_kernel, out_shape=jax.ShapeDtypeStruct((2 * planes2, c...  5.5 us
    unnamed x12, local copies, waits for them, and re-layouts  4.26 us
  transfers between devices with their start and end apart: 1, of which 1 were waited for; matrix products, arithmetic and copies ran while one was open for 2% of the time, Pallas kernels for 5%

profile of v12, /device:TPU:1, one launch (start us, length us, event | category | flops | bytes accessed | tf_op | source)
XLA Modules:
  0.0 117.3 jit_solution(6612283408670022507)
XLA Ops:
  0.6 0.0 copy-start.4
  0.6 0.0 copy-start.3
  0.7 0.0 copy-start.2
  0.7 12.0 %all-to-all-start = ((bf16[32,16,2,1024]{3,2,1,0:T(2,128)(2,1)}), bf16[32,16,2,1024]{3,2,1,0:T(2,128)(2,1)S(1)}, u32[]{:S(2)}, u32[]{:S(2)}) async-start(bf16[32,16,2,1024]{3,2,1,0:T(2,128)(2,1)} %param.7), calls=%async_computation | async-start | bytes 4194304 | tf_op jit(solution)/shard_map/all_to_all | solution.py:375
  12.7 0.0 copy-start.1
  12.7 0.0 copy-done.4
  12.7 0.7 copy.18.w1_ref
  13.4 0.0 copy-done.3
  13.4 0.8 copy.19.w2_ref
  14.2 0.0 copy-done.2
  14.2 0.9 reshape_squeeze.3.ogn_ref
  15.0 0.1 copy.16
  15.1 0.2 copy.17
  15.3 0.2 reshape.29.w2t_ref
  15.5 0.0 copy-done.1
  15.5 5.5 %shard_map.94.act_ref = bf16[32,32,256]{2,1,0:T(8,128)(2,1)S(1)} custom-call(bf16[1024,64]{1,0:T(8,128)(2,1)S(1)} %bitcast.26, bf16[3,32,576]{2,1,0:T(8,128)(2,1)S(1)} %reshape.29.w2t_ref, bf16[64,2304]{1,0:T(8,128)(2,1)S(1)} %copy-done.1), custom_call_target="tpu_custom_call" | custom-call | flops 1207959552 | bytes 1060864 | tf_op jit(solution)/shard_map/pallas_call | solution.py:69
  21.0 0.0 copy-start
  21.0 0.8 copy-done
  21.8 39.3 %all-to-all-done = bf16[32,16,2,1024]{3,2,1,0:T(2,128)(2,1)S(1)} async-done(((bf16[32,16,2,1024]{3,2,1,0:T(2,128)(2,1)}), bf16[32,16,2,1024]{3,2,1,0:T(2,128)(2,1)S(1)}, u32[]{:S(2)}, u32[]{:S(2)}) %all-to-all-start) | async-done | bytes 2097184 | tf_op jit(solution)/shard_map/all_to_all | solution.py:375
  61.2 2.0 %copy.15 = bf16[1,16,32,2,1024]{4,1,3,2,0:T(8,128)(2,1)} copy(bf16[1,16,32,2,1024]{4,3,1,2,0:T(2,128)(2,1)S(1)} %bitcast.28) | data formatting | bytes 4194304 | tf_op jit(solution)/shard_map/all_to_all | solution.py:375
  63.2 14.2 %shard_map.95 = (bf16[64,16,64]{2,1,0:T(8,128)(2,1)}, f32[32,432]{1,0:T(8,128)}, f32[64,864]{1,0:T(8,128)}) custom-call(bf16[64,16,1024]{2,1,0:T(8,128)(2,1)} %bitcast.27, bf16[64,1024]{1,0:T(8,128)(2,1)} %reshape_squeeze.3.ogn_ref, bf16[32,32,256]{2,1,0:T(8,128)(2,1)} %copy-done, bf16[32,432]{1,0:T(8,128)(2,1)} %copy.18.w1_ref, ...), custom_call_target="tpu_custom_call" | custom-call | tf_op jit(solution)/shard_map/pallas_call | solution.py:158
  77.4 36.5 %shard_map.96 = (f32[432,32]{1,0:T(8,128)}, f32[864,64]{1,0:T(8,128)}) custom-call(f32[32,432]{1,0:T(8,128)} %get-tuple-element.9.g1_ref, f32[64,864]{1,0:T(8,128)} %get-tuple-element.10.g2_ref), custom_call_target="tpu_custom_call" | custom-call | tf_op jit(solution)/shard_map/pallas_call | solution.py:351
  113.9 1.6 %copy.22 = f32[32,16,3,3,3]{0,1,4,3,2:T(8,128)} copy(f32[32,16,3,3,3]{0,1,4,3,2:T(8,128)} %bitcast.33) | data formatting | bytes 110592
  115.5 1.8 %copy.23 = f32[64,32,3,3,3]{0,1,4,3,2:T(8,128)} copy(f32[64,32,3,3,3]{0,1,4,3,2:T(8,128)} %bitcast.32) | data formatting | bytes 442368
Async XLA Ops:
  0.6 12.1 %copy-start.4 = (bf16[32,16,3,3,3]{0,1,4,3,2:T(8,128)(2,1)S(1)}, bf16[32,16,3,3,3]{0,1,4,3,2:T(8,128)(2,1)}, u32[]{:S(2)}) copy-start(bf16[32,16,3,3,3]{0,1,4,3,2:T(8,128)(2,1)} %param.8) | copy-start | bytes 82948
  0.6 12.8 %copy-start.3 = (bf16[64,32,3,3,3]{0,1,4,3,2:T(8,128)(2,1)S(1)}, bf16[64,32,3,3,3]{0,1,4,3,2:T(8,128)(2,1)}, u32[]{:S(2)}) copy-start(bf16[64,32,3,3,3]{0,1,4,3,2:T(8,128)(2,1)} %param.9) | copy-start | bytes 331780
  0.7 13.5 %copy-start.2 = (bf16[1,64,16,64]{3,2,1,0:T(8,128)(2,1)S(1)}, bf16[1,64,16,64]{3,2,1,0:T(8,128)(2,1)}, u32[]{:S(2)}) copy-start(bf16[1,64,16,64]{3,2,1,0:T(8,128)(2,1)} %param.10) | copy-start | bytes 393220
  0.7 60.5 %all-to-all-start = ((bf16[32,16,2,1024]{3,2,1,0:T(2,128)(2,1)}), bf16[32,16,2,1024]{3,2,1,0:T(2,128)(2,1)S(1)}, u32[]{:S(2)}, u32[]{:S(2)}) async-start(bf16[32,16,2,1024]{3,2,1,0:T(2,128)(2,1)} %param.7), calls=%async_computation | async-start | bytes 4194304 | tf_op jit(solution)/shard_map/all_to_all | solution.py:375
  12.7 2.8 %copy-start.1 = (bf16[64,2304]{1,0:T(8,128)(2,1)S(1)}, bf16[64,2304]{1,0:T(8,128)(2,1)}, u32[]{:S(2)}) copy-start(bf16[64,2304]{1,0:T(8,128)(2,1)} %constant.6.clone.up_ref) | copy-start | bytes 884740
  21.0 0.8 copy-start

commit v13 on v12

--- a/solution.py
+++ b/solution.py
@@ -115,7 +115,7 @@
         a2_ref[pd + 1] = (pre * sig).astype(a2_ref.dtype)
         return carry
 
-    lax.fori_loop(0, planes1, build_plane, 0, unroll=4)
+    lax.fori_loop(0, planes1, build_plane, 0, unroll=8)
 
     a2 = a2_ref[...].reshape((planes1 + 1) * c1, plane1)
     for bc in range(9):
@@ -145,7 +145,7 @@
         fg_ref[...] += lax.dot_general(pg, s_ref[d2], NT, preferred_element_type=jnp.float32)
         return carry
 
-    lax.fori_loop(0, planes1, back_plane, 0, unroll=8)
+    lax.fori_loop(0, planes1, back_plane, 0, unroll=16)
 
 
 def per_sample(x, ogn, act, w1, w2, t1, sel2):

time: 118 us -> 116 us (0.983)
  no operation moved by 1% of the time
where the time goes in v13:
time: 116 us
  Pallas kernels  55.1 us (48%)
  waiting for transfers between devices  39.3 us (34%)
  starting transfers between devices  12 us (10%)
  local copies, waits for them, and re-layouts  9.05 us (8%)
    all_to_all x1, waiting for transfers between devices, body(): lax.all_to_all(crops, 'space', split_axis=0, concat_axis=2, tiled=True)  39.3 us
    pallas_call x1, Pallas kernels, allreduce(): pl.pallas_call(functools.partial(allreduce_kernel, axis_order, rounds), o...  36.5 us
    pallas_call x1, Pallas kernels, per_sample(): pl.pallas_call(conv_kernel, out_shape=(jax.ShapeDtypeStruct((c2, planes2,...  13.1 us
    all_to_all x1, starting transfers between devices, body(): lax.all_to_all(crops, 'space', split_axis=0, concat_axis=2, tiled=True)  12 us
    pallas_call x1, Pallas kernels, act_grad_of(): pl.pallas_call(act_kernel, out_shape=jax.ShapeDtypeStruct((2 * planes2, c...  5.5 us
    unnamed x12, local copies, waits for them, and re-layouts  4.26 us
  transfers between devices with their start and end apart: 1, of which 1 were waited for; matrix products, arithmetic and copies ran while one was open for 2% of the time, Pallas kernels for 5%

profile of v13, /device:TPU:1, one launch (start us, length us, event | category | flops | bytes accessed | tf_op | source)
XLA Modules:
  0.0 116.2 jit_solution(17506332902627686748)
XLA Ops:
  0.6 0.0 copy-start.4
  0.6 0.0 copy-start.3
  0.7 0.0 copy-start.2
  0.7 12.0 %all-to-all-start = ((bf16[32,16,2,1024]{3,2,1,0:T(2,128)(2,1)}), bf16[32,16,2,1024]{3,2,1,0:T(2,128)(2,1)S(1)}, u32[]{:S(2)}, u32[]{:S(2)}) async-start(bf16[32,16,2,1024]{3,2,1,0:T(2,128)(2,1)} %param.7), calls=%async_computation | async-start | bytes 4194304 | tf_op jit(solution)/shard_map/all_to_all | solution.py:375
  12.7 0.0 copy-start.1
  12.7 0.0 copy-done.4
  12.7 0.7 copy.18.w1_ref
  13.4 0.0 copy-done.3
  13.4 0.8 copy.19.w2_ref
  14.2 0.0 copy-done.2
  14.2 0.9 reshape_squeeze.3.ogn_ref
  15.0 0.1 copy.16
  15.1 0.2 copy.17
  15.3 0.2 reshape.29.w2t_ref
  15.5 0.0 copy-done.1
  15.5 5.5 %shard_map.94.act_ref = bf16[32,32,256]{2,1,0:T(8,128)(2,1)S(1)} custom-call(bf16[1024,64]{1,0:T(8,128)(2,1)S(1)} %bitcast.26, bf16[3,32,576]{2,1,0:T(8,128)(2,1)S(1)} %reshape.29.w2t_ref, bf16[64,2304]{1,0:T(8,128)(2,1)S(1)} %copy-done.1), custom_call_target="tpu_custom_call" | custom-call | flops 1207959552 | bytes 1060864 | tf_op jit(solution)/shard_map/pallas_call | solution.py:69
  21.0 0.0 copy-start
  21.0 0.8 copy-done
  21.8 39.3 %all-to-all-done = bf16[32,16,2,1024]{3,2,1,0:T(2,128)(2,1)S(1)} async-done(((bf16[32,16,2,1024]{3,2,1,0:T(2,128)(2,1)}), bf16[32,16,2,1024]{3,2,1,0:T(2,128)(2,1)S(1)}, u32[]{:S(2)}, u32[]{:S(2)}) %all-to-all-start) | async-done | bytes 2097184 | tf_op jit(solution)/shard_map/all_to_all | solution.py:375
  61.2 2.0 %copy.15 = bf16[1,16,32,2,1024]{4,1,3,2,0:T(8,128)(2,1)} copy(bf16[1,16,32,2,1024]{4,3,1,2,0:T(2,128)(2,1)S(1)} %bitcast.28) | data formatting | bytes 4194304 | tf_op jit(solution)/shard_map/all_to_all | solution.py:375
  63.2 13.1 %shard_map.95 = (bf16[64,16,64]{2,1,0:T(8,128)(2,1)}, f32[32,432]{1,0:T(8,128)}, f32[64,864]{1,0:T(8,128)}) custom-call(bf16[64,16,1024]{2,1,0:T(8,128)(2,1)} %bitcast.27, bf16[64,1024]{1,0:T(8,128)(2,1)} %reshape_squeeze.3.ogn_ref, bf16[32,32,256]{2,1,0:T(8,128)(2,1)} %copy-done, bf16[32,432]{1,0:T(8,128)(2,1)} %copy.18.w1_ref, ...), custom_call_target="tpu_custom_call" | custom-call | tf_op jit(solution)/shard_map/pallas_call | solution.py:158
  76.3 36.5 %shard_map.96 = (f32[432,32]{1,0:T(8,128)}, f32[864,64]{1,0:T(8,128)}) custom-call(f32[32,432]{1,0:T(8,128)} %get-tuple-element.9.g1_ref, f32[64,864]{1,0:T(8,128)} %get-tuple-element.10.g2_ref), custom_call_target="tpu_custom_call" | custom-call | tf_op jit(solution)/shard_map/pallas_call | solution.py:351
  112.8 1.6 %copy.22 = f32[32,16,3,3,3]{0,1,4,3,2:T(8,128)} copy(f32[32,16,3,3,3]{0,1,4,3,2:T(8,128)} %bitcast.33) | data formatting | bytes 110592
  114.4 1.8 %copy.23 = f32[64,32,3,3,3]{0,1,4,3,2:T(8,128)} copy(f32[64,32,3,3,3]{0,1,4,3,2:T(8,128)} %bitcast.32) | data formatting | bytes 442368
Async XLA Ops:
  0.6 12.1 %copy-start.4 = (bf16[32,16,3,3,3]{0,1,4,3,2:T(8,128)(2,1)S(1)}, bf16[32,16,3,3,3]{0,1,4,3,2:T(8,128)(2,1)}, u32[]{:S(2)}) copy-start(bf16[32,16,3,3,3]{0,1,4,3,2:T(8,128)(2,1)} %param.8) | copy-start | bytes 82948
  0.6 12.8 %copy-start.3 = (bf16[64,32,3,3,3]{0,1,4,3,2:T(8,128)(2,1)S(1)}, bf16[64,32,3,3,3]{0,1,4,3,2:T(8,128)(2,1)}, u32[]{:S(2)}) copy-start(bf16[64,32,3,3,3]{0,1,4,3,2:T(8,128)(2,1)} %param.9) | copy-start | bytes 331780
  0.7 13.5 %copy-start.2 = (bf16[1,64,16,64]{3,2,1,0:T(8,128)(2,1)S(1)}, bf16[1,64,16,64]{3,2,1,0:T(8,128)(2,1)}, u32[]{:S(2)}) copy-start(bf16[1,64,16,64]{3,2,1,0:T(8,128)(2,1)} %param.10) | copy-start | bytes 393220
  0.7 60.5 %all-to-all-start = ((bf16[32,16,2,1024]{3,2,1,0:T(2,128)(2,1)}), bf16[32,16,2,1024]{3,2,1,0:T(2,128)(2,1)S(1)}, u32[]{:S(2)}, u32[]{:S(2)}) async-start(bf16[32,16,2,1024]{3,2,1,0:T(2,128)(2,1)} %param.7), calls=%async_computation | async-start | bytes 4194304 | tf_op jit(solution)/shard_map/all_to_all | solution.py:375
  12.7 2.8 %copy-start.1 = (bf16[64,2304]{1,0:T(8,128)(2,1)S(1)}, bf16[64,2304]{1,0:T(8,128)(2,1)}, u32[]{:S(2)}) copy-start(bf16[64,2304]{1,0:T(8,128)(2,1)} %constant.6.clone.up_ref) | copy-start | bytes 884740
  21.0 0.8 copy-start

commit v14 on v13

--- a/solution.py
+++ b/solution.py
@@ -118,9 +118,8 @@
     lax.fori_loop(0, planes1, build_plane, 0, unroll=8)
 
     a2 = a2_ref[...].reshape((planes1 + 1) * c1, plane1)
-    for bc in range(9):
-        q2 = jnp.dot(a2, sel2_ref[:, bc * 128:(bc + 1) * 128], preferred_element_type=jnp.float32)
-        q2_ref[:, :, bc * 128:(bc + 1) * 128] = q2.reshape(planes1 + 1, c1, 128)
+    q2 = jnp.dot(a2, sel2_ref[...], preferred_element_type=jnp.float32)
+    q2_ref[...] = q2.reshape(planes1 + 1, c1, 9 * 128)
 
     sg_ref[...] = jnp.zeros(sg_ref.shape, sg_ref.dtype)
     for n in range(planes2 // 2):

time: 116 us -> 116 us (level)
  no operation moved by 1% of the time
where the time goes in v14:
time: 116 us
  Pallas kernels  54.5 us (47%)
  waiting for transfers between devices  39.3 us (34%)
  starting transfers between devices  12 us (10%)
  local copies, waits for them, and re-layouts  9.05 us (8%)
    all_to_all x1, waiting for transfers between devices, body(): lax.all_to_all(crops, 'space', split_axis=0, concat_axis=2, tiled=True)  39.3 us
    pallas_call x1, Pallas kernels, allreduce(): pl.pallas_call(functools.partial(allreduce_kernel, axis_order, rounds), o...  36.5 us
    pallas_call x1, Pallas kernels, per_sample(): pl.pallas_call(conv_kernel, out_shape=(jax.ShapeDtypeStruct((c2, planes2,...  12.5 us
    all_to_all x1, starting transfers between devices, body(): lax.all_to_all(crops, 'space', split_axis=0, concat_axis=2, tiled=True)  12 us
    pallas_call x1, Pallas kernels, act_grad_of(): pl.pallas_call(act_kernel, out_shape=jax.ShapeDtypeStruct((2 * planes2, c...  5.5 us
    unnamed x12, local copies, waits for them, and re-layouts  4.26 us
  transfers between devices with their start and end apart: 1, of which 1 were waited for; matrix products, arithmetic and copies ran while one was open for 2% of the time, Pallas kernels for 5%

profile of v14, /device:TPU:1, one launch (start us, length us, event | category | flops | bytes accessed | tf_op | source)
XLA Modules:
  0.0 115.7 jit_solution(1343297286892789280)
XLA Ops:
  0.6 0.0 copy-start.4
  0.6 0.0 copy-start.3
  0.7 0.0 copy-start.2
  0.7 12.0 %all-to-all-start = ((bf16[32,16,2,1024]{3,2,1,0:T(2,128)(2,1)}), bf16[32,16,2,1024]{3,2,1,0:T(2,128)(2,1)S(1)}, u32[]{:S(2)}, u32[]{:S(2)}) async-start(bf16[32,16,2,1024]{3,2,1,0:T(2,128)(2,1)} %param.7), calls=%async_computation | async-start | bytes 4194304 | tf_op jit(solution)/shard_map/all_to_all | solution.py:374
  12.7 0.0 copy-start.1
  12.7 0.0 copy-done.4
  12.7 0.7 copy.18.w1_ref
  13.4 0.0 copy-done.3
  13.4 0.8 copy.19.w2_ref
  14.2 0.0 copy-done.2
  14.2 0.9 reshape_squeeze.3.ogn_ref
  15.0 0.1 copy.16
  15.1 0.2 copy.17
  15.3 0.2 reshape.29.w2t_ref
  15.5 0.0 copy-done.1
  15.5 5.5 %shard_map.94.act_ref = bf16[32,32,256]{2,1,0:T(8,128)(2,1)S(1)} custom-call(bf16[1024,64]{1,0:T(8,128)(2,1)S(1)} %bitcast.26, bf16[3,32,576]{2,1,0:T(8,128)(2,1)S(1)} %reshape.29.w2t_ref, bf16[64,2304]{1,0:T(8,128)(2,1)S(1)} %copy-done.1), custom_call_target="tpu_custom_call" | custom-call | flops 1207959552 | bytes 1060864 | tf_op jit(solution)/shard_map/pallas_call | solution.py:69
  21.0 0.0 copy-start
  21.0 0.8 copy-done
  21.8 39.3 %all-to-all-done = bf16[32,16,2,1024]{3,2,1,0:T(2,128)(2,1)S(1)} async-done(((bf16[32,16,2,1024]{3,2,1,0:T(2,128)(2,1)}), bf16[32,16,2,1024]{3,2,1,0:T(2,128)(2,1)S(1)}, u32[]{:S(2)}, u32[]{:S(2)}) %all-to-all-start) | async-done | bytes 2097184 | tf_op jit(solution)/shard_map/all_to_all | solution.py:374
  61.2 2.0 %copy.15 = bf16[1,16,32,2,1024]{4,1,3,2,0:T(8,128)(2,1)} copy(bf16[1,16,32,2,1024]{4,3,1,2,0:T(2,128)(2,1)S(1)} %bitcast.28) | data formatting | bytes 4194304 | tf_op jit(solution)/shard_map/all_to_all | solution.py:374
  63.2 12.5 %shard_map.95 = (bf16[64,16,64]{2,1,0:T(8,128)(2,1)}, f32[32,432]{1,0:T(8,128)}, f32[64,864]{1,0:T(8,128)}) custom-call(bf16[64,16,1024]{2,1,0:T(8,128)(2,1)} %bitcast.27, bf16[64,1024]{1,0:T(8,128)(2,1)} %reshape_squeeze.3.ogn_ref, bf16[32,32,256]{2,1,0:T(8,128)(2,1)} %copy-done, bf16[32,432]{1,0:T(8,128)(2,1)} %copy.18.w1_ref, ...), custom_call_target="tpu_custom_call" | custom-call | tf_op jit(solution)/shard_map/pallas_call | solution.py:157
  75.7 36.5 %shard_map.96 = (f32[432,32]{1,0:T(8,128)}, f32[864,64]{1,0:T(8,128)}) custom-call(f32[32,432]{1,0:T(8,128)} %get-tuple-element.9.g1_ref, f32[64,864]{1,0:T(8,128)} %get-tuple-element.10.g2_ref), custom_call_target="tpu_custom_call" | custom-call | tf_op jit(solution)/shard_map/pallas_call | solution.py:350
  112.2 1.6 %copy.22 = f32[32,16,3,3,3]{0,1,4,3,2:T(8,128)} copy(f32[32,16,3,3,3]{0,1,4,3,2:T(8,128)} %bitcast.33) | data formatting | bytes 110592
  113.8 1.8 %copy.23 = f32[64,32,3,3,3]{0,1,4,3,2:T(8,128)} copy(f32[64,32,3,3,3]{0,1,4,3,2:T(8,128)} %bitcast.32) | data formatting | bytes 442368
Async XLA Ops:
  0.6 12.1 %copy-start.4 = (bf16[32,16,3,3,3]{0,1,4,3,2:T(8,128)(2,1)S(1)}, bf16[32,16,3,3,3]{0,1,4,3,2:T(8,128)(2,1)}, u32[]{:S(2)}) copy-start(bf16[32,16,3,3,3]{0,1,4,3,2:T(8,128)(2,1)} %param.8) | copy-start | bytes 82948
  0.6 12.8 %copy-start.3 = (bf16[64,32,3,3,3]{0,1,4,3,2:T(8,128)(2,1)S(1)}, bf16[64,32,3,3,3]{0,1,4,3,2:T(8,128)(2,1)}, u32[]{:S(2)}) copy-start(bf16[64,32,3,3,3]{0,1,4,3,2:T(8,128)(2,1)} %param.9) | copy-start | bytes 331780
  0.7 13.5 %copy-start.2 = (bf16[1,64,16,64]{3,2,1,0:T(8,128)(2,1)S(1)}, bf16[1,64,16,64]{3,2,1,0:T(8,128)(2,1)}, u32[]{:S(2)}) copy-start(bf16[1,64,16,64]{3,2,1,0:T(8,128)(2,1)} %param.10) | copy-start | bytes 393220
  0.7 60.5 %all-to-all-start = ((bf16[32,16,2,1024]{3,2,1,0:T(2,128)(2,1)}), bf16[32,16,2,1024]{3,2,1,0:T(2,128)(2,1)S(1)}, u32[]{:S(2)}, u32[]{:S(2)}) async-start(bf16[32,16,2,1024]{3,2,1,0:T(2,128)(2,1)} %param.7), calls=%async_computation | async-start | bytes 4194304 | tf_op jit(solution)/shard_map/all_to_all | solution.py:374
  12.7 2.8 %copy-start.1 = (bf16[64,2304]{1,0:T(8,128)(2,1)S(1)}, bf16[64,2304]{1,0:T(8,128)(2,1)}, u32[]{:S(2)}) copy-start(bf16[64,2304]{1,0:T(8,128)(2,1)} %constant.6.clone.up_ref) | copy-start | bytes 884740
  21.0 0.8 copy-start

commit v15 on v14

--- a/solution.py
+++ b/solution.py
@@ -115,7 +115,7 @@
         a2_ref[pd + 1] = (pre * sig).astype(a2_ref.dtype)
         return carry
 
-    lax.fori_loop(0, planes1, build_plane, 0, unroll=8)
+    lax.fori_loop(0, planes1, build_plane, 0, unroll=32)
 
     a2 = a2_ref[...].reshape((planes1 + 1) * c1, plane1)
     q2 = jnp.dot(a2, sel2_ref[...], preferred_element_type=jnp.float32)
@@ -144,7 +144,7 @@
         fg_ref[...] += lax.dot_general(pg, s_ref[d2], NT, preferred_element_type=jnp.float32)
         return carry
 
-    lax.fori_loop(0, planes1, back_plane, 0, unroll=16)
+    lax.fori_loop(0, planes1, back_plane, 0, unroll=32)
 
 
 def per_sample(x, ogn, act, w1, w2, t1, sel2):

time: 116 us -> 114 us (0.983)
  Pallas kernels: 54.5 us -> 52.3 us
    pallas_call x1, Pallas kernels: 12.5 us -> 10.3 us  [per_sample(): pl.pallas_call(conv_kernel, out_shape=(jax.ShapeDtypeStruct((c2, planes2,...]
where the time goes in v15:
time: 114 us; the launch traced here: 113 us
  Pallas kernels  52.3 us (46%)
  waiting for transfers between devices  39.3 us (34%)
  starting transfers between devices  12 us (11%)
  local copies, waits for them, and re-layouts  9.05 us (8%)
    all_to_all x1, waiting for transfers between devices, body(): lax.all_to_all(crops, 'space', split_axis=0, concat_axis=2, tiled=True)  39.3 us
    pallas_call x1, Pallas kernels, allreduce(): pl.pallas_call(functools.partial(allreduce_kernel, axis_order, rounds), o...  36.5 us
    all_to_all x1, starting transfers between devices, body(): lax.all_to_all(crops, 'space', split_axis=0, concat_axis=2, tiled=True)  12 us
    pallas_call x1, Pallas kernels, per_sample(): pl.pallas_call(conv_kernel, out_shape=(jax.ShapeDtypeStruct((c2, planes2,...  10.3 us
    pallas_call x1, Pallas kernels, act_grad_of(): pl.pallas_call(act_kernel, out_shape=jax.ShapeDtypeStruct((2 * planes2, c...  5.5 us
    unnamed x12, local copies, waits for them, and re-layouts  4.26 us
  transfers between devices with their start and end apart: 1, of which 1 were waited for; matrix products, arithmetic and copies ran while one was open for 2% of the time, Pallas kernels for 5%

profile of v15, /device:TPU:1, one launch (start us, length us, event | category | flops | bytes accessed | tf_op | source)
XLA Modules:
  0.0 113.4 jit_solution(14043429479585723368)
XLA Ops:
  0.6 0.0 copy-start.4
  0.6 0.0 copy-start.3
  0.7 0.0 copy-start.2
  0.7 12.0 %all-to-all-start = ((bf16[32,16,2,1024]{3,2,1,0:T(2,128)(2,1)}), bf16[32,16,2,1024]{3,2,1,0:T(2,128)(2,1)S(1)}, u32[]{:S(2)}, u32[]{:S(2)}) async-start(bf16[32,16,2,1024]{3,2,1,0:T(2,128)(2,1)} %param.7), calls=%async_computation | async-start | bytes 4194304 | tf_op jit(solution)/shard_map/all_to_all | solution.py:374
  12.7 0.0 copy-start.1
  12.7 0.0 copy-done.4
  12.7 0.7 copy.18.w1_ref
  13.4 0.0 copy-done.3
  13.4 0.8 copy.19.w2_ref
  14.2 0.0 copy-done.2
  14.2 0.9 reshape_squeeze.3.ogn_ref
  15.0 0.1 copy.16
  15.1 0.2 copy.17
  15.3 0.2 reshape.29.w2t_ref
  15.5 0.0 copy-done.1
  15.5 5.5 %shard_map.94.act_ref = bf16[32,32,256]{2,1,0:T(8,128)(2,1)S(1)} custom-call(bf16[1024,64]{1,0:T(8,128)(2,1)S(1)} %bitcast.26, bf16[3,32,576]{2,1,0:T(8,128)(2,1)S(1)} %reshape.29.w2t_ref, bf16[64,2304]{1,0:T(8,128)(2,1)S(1)} %copy-done.1), custom_call_target="tpu_custom_call" | custom-call | flops 1207959552 | bytes 1060864 | tf_op jit(solution)/shard_map/pallas_call | solution.py:69
  21.0 0.0 copy-start
  21.0 0.8 copy-done
  21.8 39.3 %all-to-all-done = bf16[32,16,2,1024]{3,2,1,0:T(2,128)(2,1)S(1)} async-done(((bf16[32,16,2,1024]{3,2,1,0:T(2,128)(2,1)}), bf16[32,16,2,1024]{3,2,1,0:T(2,128)(2,1)S(1)}, u32[]{:S(2)}, u32[]{:S(2)}) %all-to-all-start) | async-done | bytes 2097184 | tf_op jit(solution)/shard_map/all_to_all | solution.py:374
  61.2 2.0 %copy.15 = bf16[1,16,32,2,1024]{4,1,3,2,0:T(8,128)(2,1)} copy(bf16[1,16,32,2,1024]{4,3,1,2,0:T(2,128)(2,1)S(1)} %bitcast.28) | data formatting | bytes 4194304 | tf_op jit(solution)/shard_map/all_to_all | solution.py:374
  63.2 10.3 %shard_map.95 = (bf16[64,16,64]{2,1,0:T(8,128)(2,1)}, f32[32,432]{1,0:T(8,128)}, f32[64,864]{1,0:T(8,128)}) custom-call(bf16[64,16,1024]{2,1,0:T(8,128)(2,1)} %bitcast.27, bf16[64,1024]{1,0:T(8,128)(2,1)} %reshape_squeeze.3.ogn_ref, bf16[32,32,256]{2,1,0:T(8,128)(2,1)} %copy-done, bf16[32,432]{1,0:T(8,128)(2,1)} %copy.18.w1_ref, ...), custom_call_target="tpu_custom_call" | custom-call | tf_op jit(solution)/shard_map/pallas_call | solution.py:157
  73.4 36.5 %shard_map.96 = (f32[432,32]{1,0:T(8,128)}, f32[864,64]{1,0:T(8,128)}) custom-call(f32[32,432]{1,0:T(8,128)} %get-tuple-element.9.g1_ref, f32[64,864]{1,0:T(8,128)} %get-tuple-element.10.g2_ref), custom_call_target="tpu_custom_call" | custom-call | tf_op jit(solution)/shard_map/pallas_call | solution.py:350
  110.0 1.6 %copy.22 = f32[32,16,3,3,3]{0,1,4,3,2:T(8,128)} copy(f32[32,16,3,3,3]{0,1,4,3,2:T(8,128)} %bitcast.33) | data formatting | bytes 110592
  111.6 1.8 %copy.23 = f32[64,32,3,3,3]{0,1,4,3,2:T(8,128)} copy(f32[64,32,3,3,3]{0,1,4,3,2:T(8,128)} %bitcast.32) | data formatting | bytes 442368
Async XLA Ops:
  0.6 12.1 %copy-start.4 = (bf16[32,16,3,3,3]{0,1,4,3,2:T(8,128)(2,1)S(1)}, bf16[32,16,3,3,3]{0,1,4,3,2:T(8,128)(2,1)}, u32[]{:S(2)}) copy-start(bf16[32,16,3,3,3]{0,1,4,3,2:T(8,128)(2,1)} %param.8) | copy-start | bytes 82948
  0.6 12.8 %copy-start.3 = (bf16[64,32,3,3,3]{0,1,4,3,2:T(8,128)(2,1)S(1)}, bf16[64,32,3,3,3]{0,1,4,3,2:T(8,128)(2,1)}, u32[]{:S(2)}) copy-start(bf16[64,32,3,3,3]{0,1,4,3,2:T(8,128)(2,1)} %param.9) | copy-start | bytes 331780
  0.7 13.5 %copy-start.2 = (bf16[1,64,16,64]{3,2,1,0:T(8,128)(2,1)S(1)}, bf16[1,64,16,64]{3,2,1,0:T(8,128)(2,1)}, u32[]{:S(2)}) copy-start(bf16[1,64,16,64]{3,2,1,0:T(8,128)(2,1)} %param.10) | copy-start | bytes 393220
  0.7 60.5 %all-to-all-start = ((bf16[32,16,2,1024]{3,2,1,0:T(2,128)(2,1)}), bf16[32,16,2,1024]{3,2,1,0:T(2,128)(2,1)S(1)}, u32[]{:S(2)}, u32[]{:S(2)}) async-start(bf16[32,16,2,1024]{3,2,1,0:T(2,128)(2,1)} %param.7), calls=%async_computation | async-start | bytes 4194304 | tf_op jit(solution)/shard_map/all_to_all | solution.py:374
  12.7 2.8 %copy-start.1 = (bf16[64,2304]{1,0:T(8,128)(2,1)S(1)}, bf16[64,2304]{1,0:T(8,128)(2,1)}, u32[]{:S(2)}) copy-start(bf16[64,2304]{1,0:T(8,128)(2,1)} %constant.6.clone.up_ref) | copy-start | bytes 884740
  21.0 0.8 copy-start
